TPU v7x, 256 devices: a whole 4x4x8 slice. The times are simulated.
256 devices in a mesh: seq: 64 (over x_lo, y, z), chan: 4 (over x_hi, core).
Axes of the slice: x: 4 (x_hi: 2, x_lo: 2; x = x_hi * 2 + x_lo), y: 4, z: 8, core: 2. Of those that a mesh axis runs over, the one named last changes fastest.
Arguments:
- query_proj: bfloat16 [8192, 4096], P('seq', 'chan'), may hold values from -6 to 6
- key_proj: bfloat16 [8192, 4096], P('seq', 'chan'), may hold values from -6 to 6
- value_proj: bfloat16 [8192, 4096], P('seq', 'chan'), may hold values from -6 to 6
- short_taps: float32 [3, 3, 4096], P(None, None, 'chan'), may hold values from -2.5 to 2.5
- skip_gain: float32 [4096], P('chan'), may hold values from 0.5 to 1.5
- long_filter: float32 [4096, 8192], P(('chan', 'seq')), may hold values from -1024 to 1024
- out_grad: bfloat16 [8192, 4096], P('seq', 'chan'), may hold values from -6 to 6
Outputs:
- mixed_out: bfloat16 [8192, 4096], P('seq', 'chan')
- query_grad: bfloat16 [8192, 4096], P('seq', 'chan')
- key_grad: bfloat16 [8192, 4096], P('seq', 'chan')
- value_grad: bfloat16 [8192, 4096], P('seq', 'chan')
- filter_grad: float32 [4096, 8192], P(('chan', 'seq'))
All inputs are finite; a program needn't handle non-finite values.
Results may differ from a plain program's by a relative error of at most 0.0075.
Values may be sent and summed in bfloat16 or wider, within the bound.
No kernel may reach another device: no remote copies, remote signals or barrier semaphores. Data moves between devices by JAX's collectives and lax.ppermute only.
A program may use at most 64 MiB of HBM per device.

v0:
```python
import math

import jax
import jax.numpy as jnp
import ml_dtypes
import numpy as np
from jax import lax
from jax.experimental import pallas as pl
from jax.experimental.pallas import tpu as pltpu
from jax.sharding import PartitionSpec as P

F32 = jnp.float32
BF16 = jnp.bfloat16


def passed_along(array, axis, by):
    length = lax.axis_size(axis)
    pairs = [(i, i + by) for i in range(length) if 0 <= i + by < length]
    return lax.ppermute(array, axis, pairs)


def to_mirror(array):
    count = lax.axis_size("seq") * lax.axis_size("chan")
    return lax.ppermute(array, ("seq", "chan"), [(i, count - 1 - i) for i in range(count)])


def split_bf16(matrix):
    high = matrix.astype(ml_dtypes.bfloat16)
    low = (matrix - high.astype(np.float64)).astype(ml_dtypes.bfloat16)
    return high, low


def make_tables(shards, width):
    n1 = np.arange(shards)[:, None]
    k1 = np.arange(shards)[None, :] + 0.5
    n2 = np.arange(width)
    outer = 2.0 * np.pi * k1.T * n1.T / (2 * shards)
    first = np.concatenate([np.cos(outer), -np.sin(outer)], 0)
    high, low = split_bf16(first)
    first_twice = np.concatenate([high, low], 1)
    first_thrice = np.concatenate([high, low, high], 1)
    last = first.T / (shards * width)
    high, low = split_bf16(last)
    last_twice = np.concatenate([high, low], 1)
    twist = 2.0 * np.pi * k1.T * n2[None, :] / (2 * shards * width)
    twist = np.stack([np.cos(twist), np.sin(twist)]).astype(np.float32)
    inner = 2.0 * np.pi * (n2[:, None] * n2[None, :] % width) / width
    cos, sin = np.cos(inner), np.sin(inner)
    forth = np.block([[cos, -sin], [sin, cos]]).astype(ml_dtypes.bfloat16)
    forth_conj = np.block([[cos, sin], [sin, -cos]]).astype(ml_dtypes.bfloat16)
    back = np.block([[cos, sin], [-sin, cos]]).astype(ml_dtypes.bfloat16)
    back_conj = np.block([[cos, sin], [sin, -cos]]).astype(ml_dtypes.bfloat16)
    return dict(
        first_twice=first_twice,
        first_thrice=first_thrice,
        last_twice=last_twice,
        twist=twist,
        forth=forth,
        kernel_forth=np.concatenate([forth, forth_conj], 0),
        back=back,
        back_both=np.concatenate([back, back_conj], 1),
    )


def dot(left, right):
    return jnp.dot(left, right, preferred_element_type=F32)


def call(kernel, out_shape, scratch=(), flops=0, bytes_accessed=0, **more):
    return pl.pallas_call(
        kernel,
        out_shape=out_shape,
        scratch_shapes=list(scratch),
        compiler_params=pltpu.CompilerParams(vmem_limit_bytes=48 << 20),
        cost_estimate=pl.CostEstimate(
            flops=flops, bytes_accessed=bytes_accessed, transcendentals=0
        ),
        **more,
    )


def pre_kernel(q_ref, k_ref, v_ref, g_ref, halo_ref, taps_ref, qs_ref, ks_ref, vs_ref, send_ref, ext):
    rows, channels = q_ref.shape
    group = send_ref.shape[1] // 2
    for lane in range(0, channels, 128):
        lanes = pl.ds(lane, 128)
        shorts = []
        for p, ref in enumerate((q_ref, k_ref, v_ref)):
            ext[p, 0:8, :] = halo_ref[p, :, lanes]
            ext[p, 8 : rows + 8, :] = ref[:, lanes].astype(F32)
            shorts.append(
                (
                    taps_ref[p, 0:1, lanes] * ext[p, 8 : rows + 8, :]
                    + taps_ref[p, 1:2, lanes] * ext[p, 7 : rows + 7, :]
                    + taps_ref[p, 2:3, lanes] * ext[p, 6 : rows + 6, :]
                ).astype(BF16)
            )
        qs, ks, vs = shorts
        qs_ref[:, lanes] = qs
        ks_ref[:, lanes] = ks
        vs_ref[:, lanes] = vs
        product = ks.astype(F32) * vs.astype(F32)
        gate = g_ref[:, lanes].astype(F32) * qs.astype(F32)
        blocks = pl.ds(lane // group, 128 // group)
        send_ref[blocks, 0:group, :] = product.T.astype(BF16).reshape(128 // group, group, rows)
        send_ref[blocks, group:, :] = gate.T.astype(BF16).reshape(128 // group, group, rows)


def spectrum_kernel(own_ref, mir_ref, first_ref, twist_ref, forth_ref, out_ref, own_s, mir_s, lhs):
    channels, length = own_ref.shape
    shards = twist_ref.shape[1]
    width = length // shards
    scale = 1.0 / math.sqrt(length)
    for n1 in range(shards):
        own_s[n1 * channels : (n1 + 1) * channels, :] = own_ref[:, n1 * width : (n1 + 1) * width]
        mir_s[n1 * channels : (n1 + 1) * channels, :] = mir_ref[:, n1 * width : (n1 + 1) * width].astype(F32)
    cos, sin = twist_ref[0], twist_ref[1]
    step = 4

    @pl.loop(0, channels, step=step)
    def _(base):
        for i in range(step):
            c = base + i
            own = own_s[pl.ds(c, shards, stride=channels), :]
            mir = mir_s[pl.ds(channels - 1 - c, shards, stride=channels), :].astype(BF16)
            high = own.astype(BF16)
            low = (own - high.astype(F32)).astype(BF16)
            part = dot(first_ref[...], jnp.concatenate([high, high, low], 0))
            real, imag = part[:shards], part[shards:]
            rows = pl.ds(i * shards, shards)
            lhs[rows, 0:width] = (real * cos + imag * sin).astype(BF16)
            lhs[rows, width : 2 * width] = (imag * cos - real * sin).astype(BF16)
            part = dot(first_ref[:, : 2 * shards], jnp.concatenate([mir, mir], 0))
            real, imag = part[:shards], part[shards:]
            lhs[rows, 2 * width : 3 * width] = (real * cos + imag * sin).astype(BF16)
            lhs[rows, 3 * width :] = (imag * cos - real * sin).astype(BF16)
        out_ref[pl.ds(base * shards, step * shards), :] = dot(lhs[...], forth_ref[...]) * scale


def mix_kernel(x_ref, spec_ref, skip_ref, first_ref, twist_ref, forth_ref, back_ref, last_ref, out_ref, corr_ref, xs, ys, lhs, spec):
    shards, both, width = x_ref.shape
    channels = both // 2
    xs[...] = x_ref[...].reshape(shards * both, width).astype(F32)
    cos, sin = twist_ref[0], twist_ref[1]
    step = 4

    @pl.loop(0, channels, step=step)
    def _(base):
        for i in range(step):
            c = base + i
            product = xs[pl.ds(c, shards, stride=both), :].astype(BF16)
            gate = xs[pl.ds(channels + c, shards, stride=both), :].astype(BF16)
            rhs = jnp.concatenate([product, gate], 1)
            part = dot(first_ref[...], jnp.concatenate([rhs, rhs], 0))
            for j in range(2):
                real = part[:shards, j * width : (j + 1) * width]
                imag = part[shards:, j * width : (j + 1) * width]
                rows = pl.ds((2 * i + j) * shards, shards)
                lhs[rows, :width] = (real * cos + imag * sin).astype(BF16)
                lhs[rows, width:] = (imag * cos - real * sin).astype(BF16)
        spec[...] = dot(lhs[...], forth_ref[...])
        for i in range(step):
            c = base + i
            kr = spec_ref[pl.ds(c * shards, shards), :width]
            ki = spec_ref[pl.ds(c * shards, shards), width:]
            pr = spec[2 * i * shards : (2 * i + 1) * shards, :width]
            pi = spec[2 * i * shards : (2 * i + 1) * shards, width:]
            gr = spec[(2 * i + 1) * shards : (2 * i + 2) * shards, :width]
            gi = spec[(2 * i + 1) * shards : (2 * i + 2) * shards, width:]
            rows = pl.ds(2 * i * shards, shards)
            lhs[rows, :width] = (kr * pr - ki * pi).astype(BF16)
            lhs[rows, width:] = (kr * pi + ki * pr).astype(BF16)
            rows = pl.ds((2 * i + 1) * shards, shards)
            lhs[rows, :width] = (kr * gr + ki * gi).astype(BF16)
            lhs[rows, width:] = (kr * gi - ki * gr).astype(BF16)
            rows = pl.ds(c * shards, shards)
            corr_ref[rows, :width] = (pr * gr + pi * gi).astype(BF16)
            corr_ref[rows, width:] = (pr * gi - pi * gr).astype(BF16)
        spec[...] = dot(lhs[...], back_ref[...])
        for i in range(step):
            c = base + i
            columns = []
            for j in range(2):
                real = spec[(2 * i + j) * shards : (2 * i + j + 1) * shards, :width]
                imag = spec[(2 * i + j) * shards : (2 * i + j + 1) * shards, width:]
                columns.append(
                    jnp.concatenate(
                        [(real * cos - imag * sin).astype(BF16), (imag * cos + real * sin).astype(BF16)], 0
                    )
                )
            rhs = jnp.concatenate(columns, 1)
            part = dot(last_ref[...], jnp.concatenate([rhs, rhs], 0))
            skip = skip_ref[c]
            for j in range(2):
                place = pl.ds(j * channels + c, shards, stride=both)
                ys[place, :] = part[:, j * width : (j + 1) * width] + skip * xs[place, :]

    out_ref[...] = ys[...].astype(BF16).reshape(shards, both, width)


def corr_kernel(corr_ref, twist_ref, back_ref, last_ref, own_ref, mir_ref, own_s, mir_s, spec):
    channels, length = own_ref.shape
    shards = twist_ref.shape[1]
    width = length // shards
    scale = 1.0 / math.sqrt(length)
    cos, sin = twist_ref[0], twist_ref[1]
    step = 4

    @pl.loop(0, channels, step=step)
    def _(base):
        spec[...] = dot(corr_ref[pl.ds(base * shards, step * shards), :], back_ref[...])
        for i in range(step):
            c = base + i
            columns = []
            for j in range(2):
                real = spec[i * shards : (i + 1) * shards, 2 * j * width : (2 * j + 1) * width]
                imag = spec[i * shards : (i + 1) * shards, (2 * j + 1) * width : (2 * j + 2) * width]
                columns.append(
                    jnp.concatenate(
                        [(real * cos - imag * sin).astype(BF16), (imag * cos + real * sin).astype(BF16)], 0
                    )
                )
            rhs = jnp.concatenate(columns, 1)
            part = dot(last_ref[...], jnp.concatenate([rhs, rhs], 0)) * scale
            own_s[pl.ds(c, shards, stride=channels), :] = part[:, :width]
            mir_s[pl.ds(channels - 1 - c, shards, stride=channels), :] = part[:, width:]

    for n1 in range(shards):
        own_ref[:, n1 * width : (n1 + 1) * width] = own_s[n1 * channels : (n1 + 1) * channels, :]
        mir_ref[:, n1 * width : (n1 + 1) * width] = mir_s[n1 * channels : (n1 + 1) * channels, :].astype(BF16)


def head_kernel(r_ref, g_ref, ks_ref, vs_ref, out_ref):
    blocks, both, width = r_ref.shape
    group = both // 2
    channels = blocks * group
    pick = (
        lax.broadcasted_iota(jnp.int32, (8, width), 0) == lax.broadcasted_iota(jnp.int32, (8, width), 1)
    ).astype(BF16)
    across = (((1,), (1,)), ((), ()))
    mix = lax.dot_general(pick, r_ref[:, :group, :].reshape(channels, width), across, preferred_element_type=F32)
    back = lax.dot_general(pick, r_ref[:, group:, :].reshape(channels, width), across, preferred_element_type=F32)
    out_ref[0] = g_ref[0:8, :].astype(F32) * mix
    out_ref[1] = back * vs_ref[0:8, :].astype(F32)
    out_ref[2] = back * ks_ref[0:8, :].astype(F32)


def post_kernel(r_ref, g_ref, qs_ref, ks_ref, vs_ref, taps_ref, mixed_ref, q_ref, k_ref, v_ref, tail_ref, ext):
    rows, channels = g_ref.shape
    group = r_ref.shape[1] // 2
    for lane in range(0, channels, 128):
        lanes = pl.ds(lane, 128)
        blocks = pl.ds(lane // group, 128 // group)
        mix = r_ref[blocks, :group, :].reshape(128, rows).astype(F32).T
        back = r_ref[blocks, group:, :].reshape(128, rows).astype(F32).T
        mixed_ref[:, lanes] = (qs_ref[:, lanes].astype(F32) * mix).astype(BF16)
        parts = (
            g_ref[:, lanes].astype(F32) * mix,
            back * vs_ref[:, lanes].astype(F32),
            back * ks_ref[:, lanes].astype(F32),
        )
        for p, ref in enumerate((q_ref, k_ref, v_ref)):
            ext[p, 0:rows, :] = parts[p]
            tail_ref[p, :, lanes] = parts[p][rows - 16 :]
            ref[:, lanes] = (
                taps_ref[p, 0:1, lanes] * parts[p]
                + taps_ref[p, 1:2, lanes] * ext[p, 1 : rows + 1, :]
                + taps_ref[p, 2:3, lanes] * ext[p, 2 : rows + 2, :]
            ).astype(BF16)


def tail_kernel(tail_ref, halo_ref, taps_ref, q_in, k_in, v_in, q_ref, k_ref, v_ref, ext):
    for p, ref in enumerate((q_ref, k_ref, v_ref)):
        ext[0:16, :] = tail_ref[p]
        ext[16:24, :] = halo_ref[p]
        ref[...] = (
            taps_ref[p, 0:1, :] * ext[0:16, :]
            + taps_ref[p, 1:2, :] * ext[1:17, :]
            + taps_ref[p, 2:3, :] * ext[2:18, :]
        ).astype(BF16)


def per_device(query_proj, key_proj, value_proj, short_taps, skip_gain, long_filter, out_grad):
    positions, width = query_proj.shape
    channels, length = long_filter.shape
    shards = lax.axis_size("seq")
    tables = make_tables(shards, positions)
    shape = jax.ShapeDtypeStruct
    own_skip = lax.dynamic_slice_in_dim(skip_gain, lax.axis_index("seq") * channels, channels)

    filter_far = to_mirror(long_filter.astype(BF16))

    ends = jnp.stack([x[positions - 2 :] for x in (query_proj, key_proj, value_proj)])
    previous = passed_along(ends, "seq", 1).astype(F32)
    previous = jnp.pad(previous, ((0, 0), (6, 0), (0, 0)))
    wide = shape((positions, width), BF16)
    query_short, key_short, value_short, send = call(
        pre_kernel,
        (wide, wide, wide, shape((shards, 2 * channels, positions), BF16)),
        [pltpu.VMEM((3, positions + 8, 128), F32)],
        flops=30 * positions * width,
        bytes_accessed=18 * positions * width,
    )(query_proj, key_proj, value_proj, out_grad, previous, short_taps)
    received = lax.all_to_all(send, "seq", split_axis=0, concat_axis=0, tiled=True)

    step = 4
    spectrum = call(
        spectrum_kernel,
        shape((channels * shards, 2 * positions), F32),
        [
            pltpu.VMEM((shards * channels, positions), F32),
            pltpu.VMEM((shards * channels, positions), F32),
            pltpu.VMEM((step * shards, 4 * positions), BF16),
        ],
        flops=16 * 2 * channels * shards * positions * positions,
        bytes_accessed=14 * channels * length,
    )(long_filter, filter_far, tables["first_thrice"], tables["twist"], tables["kernel_forth"])

    returned, corr = call(
        mix_kernel,
        (
            shape((shards, 2 * channels, positions), BF16),
            shape((channels * shards, 2 * positions), BF16),
        ),
        [
            pltpu.VMEM((shards * 2 * channels, positions), F32),
            pltpu.VMEM((shards * 2 * channels, positions), F32),
            pltpu.VMEM((2 * step * shards, 2 * positions), BF16),
            pltpu.VMEM((2 * step * shards, 2 * positions), F32),
        ],
        flops=32 * 2 * channels * shards * positions * positions,
        bytes_accessed=24 * channels * length,
        in_specs=[pl.BlockSpec(memory_space=pltpu.VMEM)] * 2
        + [pl.BlockSpec(memory_space=pltpu.SMEM)]
        + [pl.BlockSpec(memory_space=pltpu.VMEM)] * 5,
    )(
        received,
        spectrum,
        own_skip,
        tables["first_twice"],
        tables["twist"],
        tables["forth"],
        tables["back"],
        tables["last_twice"],
    )
    result = lax.all_to_all(returned, "seq", split_axis=0, concat_axis=0, tiled=True)

    lagged, lagged_back = call(
        corr_kernel,
        (shape((channels, length), F32), shape((channels, length), BF16)),
        [
            pltpu.VMEM((shards * channels, positions), F32),
            pltpu.VMEM((shards * channels, positions), F32),
            pltpu.VMEM((step * shards, 4 * positions), F32),
        ],
        flops=16 * 2 * channels * shards * positions * positions,
        bytes_accessed=12 * channels * length,
    )(corr, tables["twist"], tables["back_both"], tables["last_twice"])
    filter_grad = lagged + to_mirror(lagged_back).astype(F32)

    head = call(
        head_kernel,
        shape((3, 8, width), F32),
        flops=64 * positions * width,
        bytes_accessed=4 * positions * width,
    )(result, out_grad, key_short, value_short)
    following = passed_along(head, "seq", -1)
    mixed_out, query_part, key_part, value_part, tail = call(
        post_kernel,
        (wide, wide, wide, wide, shape((3, 16, width), F32)),
        [pltpu.VMEM((3, positions + 8, 128), F32)],
        flops=30 * positions * width,
        bytes_accessed=20 * positions * width,
    )(result, out_grad, query_short, key_short, value_short, short_taps)
    last = pl.BlockSpec((16, width), lambda i: (positions // 16 - 1, 0))
    whole = lambda *dims: pl.BlockSpec(dims, lambda i: (0,) * len(dims))
    query_grad, key_grad, value_grad = call(
        tail_kernel,
        (wide, wide, wide),
        [pltpu.VMEM((24, width), F32)],
        flops=30 * 16 * width,
        bytes_accessed=30 * 16 * width,
        grid=(1,),
        in_specs=[whole(3, 16, width), whole(3, 8, width), whole(3, 3, width), last, last, last],
        out_specs=[last, last, last],
        input_output_aliases={3: 0, 4: 1, 5: 2},
    )(tail, following, short_taps, query_part, key_part, value_part)
    return (mixed_out, query_grad, key_grad, value_grad, filter_grad)


def solution(mesh):
    in_specs = (
        P("seq", "chan"),
        P("seq", "chan"),
        P("seq", "chan"),
        P(None, None, "chan"),
        P("chan"),
        P(("chan", "seq"), None),
        P("seq", "chan"),
    )
    out_specs = (
        P("seq", "chan"),
        P("seq", "chan"),
        P("seq", "chan"),
        P("seq", "chan"),
        P(("chan", "seq"), None),
    )
    return jax.shard_map(
        per_device, mesh=mesh, in_specs=in_specs, out_specs=out_specs, check_vma=False
    )
```

profile of v0, /device:TPU:1, one launch (start us, length us, event | category | flops | bytes accessed | tf_op | source)
XLA Modules:
  0.0 106.7 jit_solution(11802897673725715090)
XLA Ops:
  0.6 0.7 slice_bitcast_fusion.2
  1.4 0.7 slice_bitcast_fusion
  2.1 0.0 copy-start.3
  2.1 4.5 %collective-permute-start = (bf16[3,2,1024]{2,1,0:T(2,128)(2,1)S(1)}, bf16[3,2,1024]{2,1,0:T(2,128)(2,1)S(1)}, u32[]{:S(2)}, u32[]{:S(2)}) collective-permute-start(bf16[3,2,1024]{2,1,0:T(2,128)(2,1)S(1)} %pad_maximum_fusion), channel_id=1, source_target_pairs={{0,4},{4,8},{8,12},{12,16},{16,20},{20,24},{24,28},{28,32},{32,36}... | collective-permute-start | bytes 36872 | tf_op jit(solution)/shard_map/ppermute | solution.py:19
  6.7 0.8 collective-permute-done
  7.5 0.0 copy-done.3
  7.5 0.0 copy-start
  7.5 0.9 copy-done
  8.5 0.0 copy-start.4
  8.5 0.9 copy-done.4
  9.4 0.9 copy-done.5
  10.4 0.0 copy-start.6
  10.4 0.9 copy-done.6
  11.3 1.5 %shard_map.182 = (bf16[128,1024]{1,0:T(8,128)(2,1)S(1)}, bf16[128,1024]{1,0:T(8,128)(2,1)S(1)}, bf16[128,1024]{1,0:T(8,128)(2,1)S(1)}, bf16[64,32,128]{2,1,0:T(8,128)(2,1)}) custom-call(bf16[128,1024]{1,0:T(8,128)(2,1)S(1)} %copy-done.4, bf16[128,1024]{1,0:T(8,128)(2,1)S(1)} %copy-done.5, bf16[128,1024]{1,0:T(8,128)(2,1)S(1)} %copy-done.6, ...), custom_call_target="tpu_custom_call" | custom-call | flops 3932160 | bytes 2359296 | tf_op jit(solution)/shard_map/pallas_call | solution.py:297
  12.9 0.0 copy-start.2
  12.9 14.2 %all-to-all-start = ((bf16[64,32,128]{2,1,0:T(8,128)(2,1)}), bf16[64,32,128]{2,1,0:T(8,128)(2,1)S(1)}, u32[]{:S(2)}, u32[]{:S(2)}) async-start(bf16[64,32,128]{2,1,0:T(8,128)(2,1)} %get-tuple-element.21), calls=%async_computation | async-start | bytes 1048576 | tf_op jit(solution)/shard_map/all_to_all | solution.py:304
  27.0 0.0 copy-done.2
  27.1 0.0 copy-start.7
  27.1 0.0 copy-start.8
  27.1 9.2 %collective-permute-start.1 = (bf16[16,8192]{1,0:T(8,128)(2,1)S(1)}, bf16[16,8192]{1,0:T(8,128)(2,1)S(1)}, u32[]{:S(2)}, u32[]{:S(2)}) collective-permute-start(bf16[16,8192]{1,0:T(8,128)(2,1)S(1)} %convert_element_type.9), channel_id=1, source_target_pairs={{0,255},{1,254},{2,253},{3,252},{4,251},{5,250},{6,249},{7,248},{8... | collective-permute-start | bytes 786440 | tf_op jit(solution)/shard_map/ppermute | solution.py:24
  36.3 1.3 %dynamic_slice.3.skip_ref = f32[16]{0:T(128)} dynamic-slice(f32[1024]{0:T(1024)} %param.19, s32[]{:T(128)S(6)} %select_n.3), dynamic_slice_sizes={16} | dynamic-slice | bytes 132 | tf_op jit(solution)/shard_map/dynamic_slice | solution.py:289
  37.5 19.6 %collective-permute-done.1.mir_ref = bf16[16,8192]{1,0:T(8,128)(2,1)S(1)} collective-permute-done((bf16[16,8192]{1,0:T(8,128)(2,1)S(1)}, bf16[16,8192]{1,0:T(8,128)(2,1)S(1)}, u32[]{:S(2)}, u32[]{:S(2)}) %collective-permute-start.1) | collective-permute-done | bytes 262176 | tf_op jit(solution)/shard_map/ppermute | solution.py:24
  57.1 0.0 copy-done.7
  57.1 0.0 copy-done.8
  57.1 0.8 copy-done.9
  58.0 1.9 %shard_map.183.spec_ref = f32[1024,256]{1,0:T(8,128)S(1)} custom-call(f32[16,8192]{1,0:T(8,128)S(1)} %copy-done.2, bf16[16,8192]{1,0:T(8,128)(2,1)S(1)} %collective-permute-done.1.mir_ref, bf16[128,192]{1,0:T(8,128)(2,1)S(1)} %copy-done.9, f32[2,64,128]{2,1,0:T(8,128)S(1)} %copy-done.8, bf16[512,256]{1,0:T(8,128)(2,1)S(1)} %copy-done.7), custom_call_target="tpu_custom_call" | custom-call | flops 536870912 | bytes 1835008 | tf_op jit(solution)/shard_map/pallas_call | solution.py:307
  59.9 0.0 all-to-all-done.x_ref
  59.9 0.0 copy-done.13
  59.9 0.0 copy-start.11
  59.9 0.9 copy-done.11
  60.8 0.9 copy-done.12
  61.7 0.8 copy-done.14
  62.5 0.7 copy-done.15
  63.1 5.4 %shard_map.184 = (bf16[64,32,128]{2,1,0:T(8,128)(2,1)}, bf16[1024,256]{1,0:T(8,128)(2,1)S(1)}) custom-call(bf16[64,32,128]{2,1,0:T(8,128)(2,1)S(1)} %all-to-all-done.x_ref, f32[1024,256]{1,0:T(8,128)S(1)} %shard_map.183.spec_ref, f32[16]{0:T(128)S(1)} %copy-done.15, bf16[128,128]{1,0:T(8,128)(2,1)S(1)} %copy-done.14, f32[2,64,128]{2,1,0:T(8,128)S(1)} %copy-done.8, ...), custom_call_target="tpu_custom_call" | custom-call | flops 1073741824 | bytes 3145728 | tf_op jit(solution)/shard_map/pallas_call | solution.py:319
  68.5 5.6 %all-to-all-start.1 = ((bf16[64,32,128]{2,1,0:T(8,128)(2,1)}), bf16[64,32,128]{2,1,0:T(8,128)(2,1)S(1)}, u32[]{:S(2)}, u32[]{:S(2)}) async-start(bf16[64,32,128]{2,1,0:T(8,128)(2,1)} %get-tuple-element.22), calls=%async_computation.1 | async-start | bytes 1048576 | tf_op jit(solution)/shard_map/all_to_all | solution.py:346
  74.1 0.0 copy-done.10
  74.1 0.0 copy-start.1
  74.1 1.7 %shard_map.188 = (f32[16,8192]{1,0:T(8,128)S(1)}, bf16[16,8192]{1,0:T(8,128)(2,1)S(1)}) custom-call(bf16[1024,256]{1,0:T(8,128)(2,1)S(1)} %get-tuple-element.34.corr_ref, f32[2,64,128]{2,1,0:T(8,128)S(1)} %copy-done.8, bf16[256,512]{1,0:T(8,128)(2,1)S(1)} %copy-done.10, bf16[64,256]{1,0:T(8,128)(2,1)S(1)} %copy-done.13), custom_call_target="tpu_custom_call" | custom-call | flops 536870912 | bytes 1572864 | tf_op jit(solution)/shard_map/pallas_call | solution.py:348
  75.9 5.9 %collective-permute-start.3 = (bf16[16,8192]{1,0:T(8,128)(2,1)S(1)}, bf16[16,8192]{1,0:T(8,128)(2,1)S(1)}, u32[]{:S(2)}, u32[]{:S(2)}) collective-permute-start(bf16[16,8192]{1,0:T(8,128)(2,1)S(1)} %get-tuple-element.36), channel_id=1, source_target_pairs={{0,255},{1,254},{2,253},{3,252},{4,251},{5,250},{6,249},{7,248},{8... | collective-permute-start | bytes 786440 | tf_op jit(solution)/shard_map/ppermute | solution.py:24
  81.7 10.7 %all-to-all-done.1.r_ref = bf16[64,32,128]{2,1,0:T(8,128)(2,1)S(1)} async-done(((bf16[64,32,128]{2,1,0:T(8,128)(2,1)}), bf16[64,32,128]{2,1,0:T(8,128)(2,1)S(1)}, u32[]{:S(2)}, u32[]{:S(2)}) %all-to-all-start.1) | async-done | bytes 524320 | tf_op jit(solution)/shard_map/all_to_all | solution.py:346
  92.4 0.0 copy-done.1
  92.4 0.2 shard_map.186
  92.6 1.3 %collective-permute-start.2 = (f32[3,8,1024]{2,1,0:T(8,128)S(1)}, f32[3,8,1024]{2,1,0:T(8,128)S(1)}, u32[]{:S(2)}, u32[]{:S(2)}) collective-permute-start(f32[3,8,1024]{2,1,0:T(8,128)S(1)} %shard_map.186), channel_id=1, source_target_pairs={{4,0},{8,4},{12,8},{16,12},{20,16},{24,20},{28,24},{32,28},{36,32}... | collective-permute-start | bytes 294920 | tf_op jit(solution)/shard_map/ppermute | solution.py:19
  94.0 8.7 %collective-permute-done.3 = bf16[16,8192]{1,0:T(8,128)(2,1)S(1)} collective-permute-done((bf16[16,8192]{1,0:T(8,128)(2,1)S(1)}, bf16[16,8192]{1,0:T(8,128)(2,1)S(1)}, u32[]{:S(2)}, u32[]{:S(2)}) %collective-permute-start.3) | collective-permute-done | bytes 262176 | tf_op jit(solution)/shard_map/ppermute | solution.py:24
  102.7 0.8 convert_add_fusion
  103.5 1.7 %shard_map.185 = (bf16[128,1024]{1,0:T(8,128)(2,1)}, bf16[128,1024]{1,0:T(8,128)(2,1)}, bf16[128,1024]{1,0:T(8,128)(2,1)}, bf16[128,1024]{1,0:T(8,128)(2,1)}, f32[3,16,1024]{2,1,0:T(8,128)S(1)}) custom-call(bf16[64,32,128]{2,1,0:T(8,128)(2,1)S(1)} %all-to-all-done.1.r_ref, bf16[128,1024]{1,0:T(8,128)(2,1)S(1)} %copy-done.1, ...), custom_call_target="tpu_custom_call" | custom-call | flops 3932160 | bytes 2621440 | tf_op jit(solution)/shard_map/pallas_call | solution.py:368
  105.2 0.0 collective-permute-done.2.halo_ref
  105.2 1.5 %shard_map.187 = (bf16[128,1024]{1,0:T(8,128)(2,1)}, bf16[128,1024]{1,0:T(8,128)(2,1)}, bf16[128,1024]{1,0:T(8,128)(2,1)}) custom-call(f32[3,16,1024]{2,1,0:T(8,128)S(1)} %get-tuple-element.27.tail_ref, f32[3,8,1024]{2,1,0:T(8,128)S(1)} %collective-permute-done.2.halo_ref, ...), custom_call_target="tpu_custom_call", output_to_operand_aliasing={{0}: (3, {}), {1}: (4, {}), {2}: (5, {})} | custom-call | flops 491520 | bytes 491520 | tf_op jit(solution)/shard_map/pallas_call | solution.py:377
  (10 shorter events, 0.1 us)
Async XLA Ops:
  2.1 5.4 %copy-start.3 = (f32[3,3,1024]{2,1,0:T(4,128)S(1)}, f32[3,3,1024]{2,1,0:T(4,128)}, u32[]{:S(2)}) copy-start(f32[3,3,1024]{2,1,0:T(4,128)} %taps_ref.5) | copy-start | bytes 110596
  2.1 5.3 %collective-permute-start = (bf16[3,2,1024]{2,1,0:T(2,128)(2,1)S(1)}, bf16[3,2,1024]{2,1,0:T(2,128)(2,1)S(1)}, u32[]{:S(2)}, u32[]{:S(2)}) collective-permute-start(bf16[3,2,1024]{2,1,0:T(2,128)(2,1)S(1)} %pad_maximum_fusion), channel_id=1, source_target_pairs={{0,4},{4,8},{8,12},{12,16},{16,20},{20,24},{24,28},{28,32},{32,36}... | collective-permute-start | bytes 36872 | tf_op jit(solution)/shard_map/ppermute | solution.py:19
  7.5 1.0 copy-start
  8.5 0.9 copy-start.4
  9.4 0.9 copy-start.5
  10.4 0.9 copy-start.6
  12.9 14.2 %copy-start.2 = (f32[16,8192]{1,0:T(8,128)S(1)}, f32[16,8192]{1,0:T(8,128)}, u32[]{:S(2)}) copy-start(f32[16,8192]{1,0:T(8,128)} %own_ref.1) | copy-start | bytes 1572868
  12.9 47.0 %all-to-all-start = ((bf16[64,32,128]{2,1,0:T(8,128)(2,1)}), bf16[64,32,128]{2,1,0:T(8,128)(2,1)S(1)}, u32[]{:S(2)}, u32[]{:S(2)}) async-start(bf16[64,32,128]{2,1,0:T(8,128)(2,1)} %get-tuple-element.21), calls=%async_computation | async-start | bytes 1048576 | tf_op jit(solution)/shard_map/all_to_all | solution.py:304
  27.1 30.1 %copy-start.7 = (bf16[512,256]{1,0:T(8,128)(2,1)S(1)}, bf16[512,256]{1,0:T(8,128)(2,1)}, u32[]{:S(2)}) copy-start(bf16[512,256]{1,0:T(8,128)(2,1)} %constant.33.clone.forth_ref) | copy-start | bytes 786436
  27.1 30.1 %copy-start.8 = (f32[2,64,128]{2,1,0:T(8,128)S(1)}, f32[2,64,128]{2,1,0:T(8,128)}, u32[]{:S(2)}) copy-start(f32[2,64,128]{2,1,0:T(8,128)} %constant.32.clone.twist_ref) | copy-start | bytes 196612
  27.1 30.0 %collective-permute-start.1 = (bf16[16,8192]{1,0:T(8,128)(2,1)S(1)}, bf16[16,8192]{1,0:T(8,128)(2,1)S(1)}, u32[]{:S(2)}, u32[]{:S(2)}) collective-permute-start(bf16[16,8192]{1,0:T(8,128)(2,1)S(1)} %convert_element_type.9), channel_id=1, source_target_pairs={{0,255},{1,254},{2,253},{3,252},{4,251},{5,250},{6,249},{7,248},{8... | collective-permute-start | bytes 786440 | tf_op jit(solution)/shard_map/ppermute | solution.py:24
  57.1 0.8 copy-start.9
  58.0 1.9 %copy-start.13 = (bf16[64,256]{1,0:T(8,128)(2,1)S(1)}, bf16[64,256]{1,0:T(8,128)(2,1)}, u32[]{:S(2)}) copy-start(bf16[64,256]{1,0:T(8,128)(2,1)} %constant.37.clone.last_ref) | copy-start | bytes 98308
  59.9 0.9 copy-start.11
  60.8 0.9 copy-start.12
  61.7 0.8 copy-start.14
  62.5 0.7 copy-start.15
  68.5 5.6 %copy-start.10 = (bf16[256,512]{1,0:T(8,128)(2,1)S(1)}, bf16[256,512]{1,0:T(8,128)(2,1)}, u32[]{:S(2)}) copy-start(bf16[256,512]{1,0:T(8,128)(2,1)} %constant.38.clone.back_ref) | copy-start | bytes 786436
  68.5 23.9 %all-to-all-start.1 = ((bf16[64,32,128]{2,1,0:T(8,128)(2,1)}), bf16[64,32,128]{2,1,0:T(8,128)(2,1)S(1)}, u32[]{:S(2)}, u32[]{:S(2)}) async-start(bf16[64,32,128]{2,1,0:T(8,128)(2,1)} %get-tuple-element.22), calls=%async_computation.1 | async-start | bytes 1048576 | tf_op jit(solution)/shard_map/all_to_all | solution.py:346
  74.1 18.3 %copy-start.1 = (bf16[128,1024]{1,0:T(8,128)(2,1)S(1)}, bf16[128,1024]{1,0:T(8,128)(2,1)}, u32[]{:S(2)}) copy-start(bf16[128,1024]{1,0:T(8,128)(2,1)} %g_ref.5) | copy-start | bytes 786436
  75.9 26.8 %collective-permute-start.3 = (bf16[16,8192]{1,0:T(8,128)(2,1)S(1)}, bf16[16,8192]{1,0:T(8,128)(2,1)S(1)}, u32[]{:S(2)}, u32[]{:S(2)}) collective-permute-start(bf16[16,8192]{1,0:T(8,128)(2,1)S(1)} %get-tuple-element.36), channel_id=1, source_target_pairs={{0,255},{1,254},{2,253},{3,252},{4,251},{5,250},{6,249},{7,248},{8... | collective-permute-start | bytes 786440 | tf_op jit(solution)/shard_map/ppermute | solution.py:24
  92.6 12.5 %collective-permute-start.2 = (f32[3,8,1024]{2,1,0:T(8,128)S(1)}, f32[3,8,1024]{2,1,0:T(8,128)S(1)}, u32[]{:S(2)}, u32[]{:S(2)}) collective-permute-start(f32[3,8,1024]{2,1,0:T(8,128)S(1)} %shard_map.186), channel_id=1, source_target_pairs={{4,0},{8,4},{12,8},{16,12},{20,16},{24,20},{28,24},{32,28},{36,32}... | collective-permute-start | bytes 294920 | tf_op jit(solution)/shard_map/ppermute | solution.py:19
where the time goes:
time: 108 us; the launch traced here: 107 us
  starting transfers between devices  40.6 us (38%)
  waiting for transfers between devices  39.8 us (37%)
  Pallas kernels  14 us (13%)
  local copies, waits for them, and re-layouts  10.6 us (10%)
    ppermute x2, waiting for transfers between devices, to_mirror(): lax.ppermute(array, ('seq', 'chan'), [(i, count - 1 - i) for i in range(c...  28.3 us
    ppermute x2, starting transfers between devices, to_mirror(): lax.ppermute(array, ('seq', 'chan'), [(i, count - 1 - i) for i in range(c...  15 us
    all_to_all x1, starting transfers between devices, per_device(): lax.all_to_all(send, 'seq', split_axis=0, concat_axis=0, tiled=True)  14.2 us
    all_to_all x1, waiting for transfers between devices, per_device(): lax.all_to_all(returned, 'seq', split_axis=0, concat_axis=0, tiled=True)  10.7 us
    unnamed x32, local copies, waits for them, and re-layouts  7.89 us
    ppermute x2, starting transfers between devices, passed_along(): return lax.ppermute(array, axis, pairs)  5.8 us
    all_to_all x1, starting transfers between devices, per_device(): lax.all_to_all(returned, 'seq', split_axis=0, concat_axis=0, tiled=True)  5.56 us
    pallas_call x1, Pallas kernels, per_device(): call(mix_kernel, (shape((shards, 2 * channels, positions), BF16), shape((...  5.37 us
  transfers between devices with their start and end apart: 6, of which 4 were waited for; matrix products, arithmetic and copies ran while one was open for 2% of the time, Pallas kernels for 5%

commit v1 on v0

v1 whole, which is shorter than its diff:
```python
import math

import jax
import jax.numpy as jnp
import ml_dtypes
import numpy as np
from jax import lax
from jax.experimental import pallas as pl
from jax.experimental.pallas import tpu as pltpu
from jax.sharding import PartitionSpec as P

F32 = jnp.float32
BF16 = jnp.bfloat16

SPEC_FLOPS = 1 << 34
CORR_FLOPS = 1 << 29
MIX_FLOPS = 1 << 29
ADD_FLOPS = 1 << 34


def passed_along(array, axis, by):
    length = lax.axis_size(axis)
    pairs = [(i, i + by) for i in range(length) if 0 <= i + by < length]
    return lax.ppermute(array, axis, pairs)


def to_mirror(array):
    count = lax.axis_size("seq") * lax.axis_size("chan")
    return lax.ppermute(array, ("seq", "chan"), [(i, count - 1 - i) for i in range(count)])


def split_bf16(matrix):
    high = matrix.astype(ml_dtypes.bfloat16)
    low = (matrix - high.astype(np.float64)).astype(ml_dtypes.bfloat16)
    return high, low


def make_tables(shards, width):
    n1 = np.arange(shards)[:, None]
    k1 = np.arange(shards)[None, :] + 0.5
    n2 = np.arange(width)
    outer = 2.0 * np.pi * k1.T * n1.T / (2 * shards)
    first = np.concatenate([np.cos(outer), -np.sin(outer)], 0)
    high, low = split_bf16(first)
    first_thrice = np.concatenate([high, low, high], 1)
    last = first.T / (shards * width)
    high, low = split_bf16(last)
    last_twice = np.concatenate([high, low], 1)
    twist = 2.0 * np.pi * k1.T * n2[None, :] / (2 * shards * width)
    twist = np.stack([np.cos(twist), np.sin(twist)]).astype(np.float32)
    inner = 2.0 * np.pi * (n2[:, None] * n2[None, :] % width) / width
    cos, sin = np.cos(inner), np.sin(inner)
    forth = np.block([[cos, -sin], [sin, cos]])
    conj = np.block([[cos, sin], [sin, -cos]])
    back = np.block([[cos, sin], [-sin, cos]])
    square = np.concatenate([forth, conj, back], 0).astype(ml_dtypes.bfloat16)
    first_thrice = np.pad(first_thrice, ((0, 0), (0, 2 * width - 3 * shards)))
    return np.concatenate([square, first_thrice, last_twice], 0), twist


def table_views(table_ref, shards, width):
    at = 6 * width
    return dict(
        forth=table_ref.at[0 : 2 * width],
        kernel_forth=table_ref.at[0 : 4 * width],
        conj=table_ref.at[2 * width : 4 * width],
        back=table_ref.at[4 * width : at],
        first_twice=table_ref.at[at : at + 2 * shards, : 2 * shards],
        first_thrice=table_ref.at[at : at + 2 * shards, : 3 * shards],
        last_twice=table_ref.at[at + 2 * shards : at + 3 * shards, :],
    )


def dot(left, right):
    return jnp.dot(left, right, preferred_element_type=F32)


def call(kernel, out_shape, scratch=(), flops=0, bytes_accessed=0, limit=44, **more):
    return pl.pallas_call(
        kernel,
        out_shape=out_shape,
        scratch_shapes=list(scratch),
        compiler_params=pltpu.CompilerParams(vmem_limit_bytes=limit << 20),
        cost_estimate=pl.CostEstimate(
            flops=flops, bytes_accessed=bytes_accessed, transcendentals=0
        ),
        **more,
    )


def ends_kernel(q_hbm, k_hbm, v_hbm, g_hbm, last_ref, first_ref, held, sems):
    rows = q_hbm.shape[0]
    sources = [ref.at[rows - 16 :] for ref in (q_hbm, k_hbm, v_hbm)] + [ref.at[:16] for ref in (g_hbm, k_hbm, v_hbm)]
    copies = [pltpu.make_async_copy(src, held.at[p], sems.at[p]) for p, src in enumerate(sources)]
    for copy in copies:
        copy.start()
    for p, copy in enumerate(copies):
        copy.wait()
        if p < 3:
            last_ref[p] = held[p].astype(F32)[14:16].astype(BF16)
        else:
            first_ref[p - 3] = held[p].astype(F32)[0:2].astype(BF16)


def pre_kernel(q_hbm, k_hbm, v_hbm, g_hbm, halo_ref, taps_ref, qs_ref, ks_ref, vs_ref, send_ref, ends_ref, q_ref, k_ref, v_ref, g_ref, ext, sems):
    copies = [
        pltpu.make_async_copy(src, dst, sems.at[p])
        for p, (src, dst) in enumerate(((q_hbm, q_ref), (k_hbm, k_ref), (v_hbm, v_ref), (g_hbm, g_ref)))
    ]
    for copy in copies:
        copy.start()
    for copy in copies:
        copy.wait()
    rows, channels = q_ref.shape
    group = send_ref.shape[1] // 2
    for lane in range(0, channels, 128):
        lanes = pl.ds(lane, 128)
        shorts = []
        for p, ref in enumerate((q_ref, k_ref, v_ref)):
            ext[p, 6:8, :] = halo_ref[p, :, lanes].astype(F32)
            ext[p, 8 : rows + 8, :] = ref[:, lanes].astype(F32)
            shorts.append(
                (
                    taps_ref[p, 0:1, lanes] * ext[p, 8 : rows + 8, :]
                    + taps_ref[p, 1:2, lanes] * ext[p, 7 : rows + 7, :]
                    + taps_ref[p, 2:3, lanes] * ext[p, 6 : rows + 6, :]
                ).astype(BF16)
            )
        qs, ks, vs = shorts
        qs_ref[:, lanes] = qs
        ks_ref[:, lanes] = ks
        vs_ref[:, lanes] = vs
        product = ks.astype(F32) * vs.astype(F32)
        gate = g_ref[:, lanes].astype(F32) * qs.astype(F32)
        for p in (1, 2):
            ends_ref[p - 1, :, lanes] = ext[p, rows + 6 : rows + 8, :].astype(BF16)
        blocks = pl.ds(lane // group, 128 // group)
        send_ref[blocks, 0:group, :] = product.T.astype(BF16).reshape(128 // group, group, rows)
        send_ref[blocks, group:, :] = gate.T.astype(BF16).reshape(128 // group, group, rows)


def spectrum_kernel(own_ref, mir_ref, skip_ref, table_ref, twist_ref, out_ref, own_s, mir_s, lhs):
    channels, length = own_ref.shape
    shards = twist_ref.shape[1]
    width = length // shards
    table = table_views(table_ref, shards, width)
    first_ref, forth_ref = table["first_thrice"], table["kernel_forth"]
    scale = 1.0 / math.sqrt(length)
    first_channel = lax.axis_index("seq") * channels
    for n1 in range(shards):
        own_s[n1 * channels : (n1 + 1) * channels, :] = own_ref[:, n1 * width : (n1 + 1) * width]
        mir_s[n1 * channels : (n1 + 1) * channels, :] = mir_ref[:, n1 * width : (n1 + 1) * width].astype(F32)
    cos, sin = twist_ref[0], twist_ref[1]
    step = 4

    @pl.loop(0, channels, step=step)
    def _(base):
        for i in range(step):
            c = base + i
            own = own_s[pl.ds(c, shards, stride=channels), :]
            mir = mir_s[pl.ds(channels - 1 - c, shards, stride=channels), :].astype(BF16)
            high = own.astype(BF16)
            low = (own - high.astype(F32)).astype(BF16)
            part = dot(first_ref[...], jnp.concatenate([high, high, low], 0))
            real, imag = part[:shards], part[shards:]
            rows = pl.ds(i * shards, shards)
            lhs[rows, 0:width] = (real * cos + imag * sin).astype(BF16)
            lhs[rows, width : 2 * width] = (imag * cos - real * sin).astype(BF16)
            part = dot(table["first_twice"][...], jnp.concatenate([mir, mir], 0))
            real, imag = part[:shards], part[shards:]
            lhs[rows, 2 * width : 3 * width] = (real * cos + imag * sin).astype(BF16)
            lhs[rows, 3 * width :] = (imag * cos - real * sin).astype(BF16)
        part = dot(lhs[...], forth_ref[...]) * scale
        for i in range(step):
            c = base + i
            rows = pl.ds(c * shards, shards)
            out_ref[rows, :width] = part[i * shards : (i + 1) * shards, :width] + skip_ref[first_channel + c]
            out_ref[rows, width:] = part[i * shards : (i + 1) * shards, width:]


def signals_from(spec, shards, width, cos, sin, last_ref):
    columns = []
    for real, imag in spec:
        columns.append(
            jnp.concatenate([(real * cos - imag * sin).astype(BF16), (imag * cos + real * sin).astype(BF16)], 0)
        )
    rhs = jnp.concatenate(columns, 1)
    return dot(last_ref[...], jnp.concatenate([rhs, rhs], 0))


def corr_kernel(x_ref, table_ref, twist_ref, spectra_ref, own_ref, mir_ref, xs, own_s, mir_s, lhs, spec):
    shards, both, width = x_ref.shape
    channels = both // 2
    table = table_views(table_ref, shards, width)
    first_ref, last_ref = table["first_twice"], table["last_twice"]
    scale = 1.0 / math.sqrt(shards * width)
    xs[...] = x_ref[...].reshape(shards * both, width).astype(F32)
    cos, sin = twist_ref[0], twist_ref[1]
    step = 4

    @pl.loop(0, channels, step=step)
    def _(base):
        for i in range(step):
            c = base + i
            product = xs[pl.ds(c, shards, stride=both), :].astype(BF16)
            gate = xs[pl.ds(channels + c, shards, stride=both), :].astype(BF16)
            rhs = jnp.concatenate([product, gate], 1)
            part = dot(first_ref[...], jnp.concatenate([rhs, rhs], 0))
            for j in range(2):
                real = part[:shards, j * width : (j + 1) * width]
                imag = part[shards:, j * width : (j + 1) * width]
                rows = pl.ds((2 * i + j) * shards, shards)
                lhs[rows, :width] = (real * cos + imag * sin).astype(BF16)
                lhs[rows, width:] = (imag * cos - real * sin).astype(BF16)
        both_spec = dot(lhs[...], table["forth"][...])
        spectra_ref[pl.ds(2 * base * shards, 2 * step * shards), :] = both_spec
        for i in range(step):
            pr = both_spec[2 * i * shards : (2 * i + 1) * shards, :width]
            pi = both_spec[2 * i * shards : (2 * i + 1) * shards, width:]
            gr = both_spec[(2 * i + 1) * shards : (2 * i + 2) * shards, :width]
            gi = both_spec[(2 * i + 1) * shards : (2 * i + 2) * shards, width:]
            rows = pl.ds(i * shards, shards)
            lhs[rows, :width] = (pr * gr + pi * gi).astype(BF16)
            lhs[rows, width:] = (pr * gi - pi * gr).astype(BF16)
        product = lhs[: step * shards, :]
        spec[:, : 2 * width] = dot(product, table["back"][...])
        spec[:, 2 * width :] = dot(product, table["conj"][...])
        for i in range(step):
            c = base + i
            rows = slice(i * shards, (i + 1) * shards)
            pairs = [
                (spec[rows, 2 * j * width : (2 * j + 1) * width], spec[rows, (2 * j + 1) * width : (2 * j + 2) * width])
                for j in range(2)
            ]
            part = signals_from(pairs, shards, width, cos, sin, last_ref) * scale
            own_s[pl.ds(c, shards, stride=channels), :] = part[:, :width]
            mir_s[pl.ds(channels - 1 - c, shards, stride=channels), :] = part[:, width:]

    for n1 in range(shards):
        own_ref[:, n1 * width : (n1 + 1) * width] = own_s[n1 * channels : (n1 + 1) * channels, :]
        mir_ref[:, n1 * width : (n1 + 1) * width] = mir_s[n1 * channels : (n1 + 1) * channels, :].astype(BF16)


def mix_kernel(spectra_ref, spec_ref, table_ref, twist_ref, out_ref, ys, lhs, spec, first_s, extra_s):
    shards, rows_sent, width = out_ref.shape
    channels = spec_ref.shape[0] // shards
    both = 2 * channels
    table = table_views(table_ref, shards, width)
    last_ref = table["last_twice"]
    cos, sin = twist_ref[0], twist_ref[1]
    step = 4
    lane_channel = lax.broadcasted_iota(jnp.int32, (shards, width), 1) % channels
    first_s[...] = jnp.zeros_like(first_s)

    @pl.loop(0, channels, step=step)
    def _(base):
        for i in range(step):
            c = base + i
            kr = spec_ref[pl.ds(c * shards, shards), :width]
            ki = spec_ref[pl.ds(c * shards, shards), width:]
            pr = spectra_ref[pl.ds(2 * c * shards, shards), :width]
            pi = spectra_ref[pl.ds(2 * c * shards, shards), width:]
            gr = spectra_ref[pl.ds((2 * c + 1) * shards, shards), :width]
            gi = spectra_ref[pl.ds((2 * c + 1) * shards, shards), width:]
            rows = pl.ds(2 * i * shards, shards)
            lhs[rows, :width] = (kr * pr - ki * pi).astype(BF16)
            lhs[rows, width:] = (kr * pi + ki * pr).astype(BF16)
            rows = pl.ds((2 * i + 1) * shards, shards)
            lhs[rows, :width] = (kr * gr + ki * gi).astype(BF16)
            lhs[rows, width:] = (kr * gi - ki * gr).astype(BF16)
        spec[...] = dot(lhs[...], table["back"][...])
        firsts = [jnp.zeros((shards, width), F32)] * 4
        for i in range(step):
            c = base + i
            pairs = []
            for j in range(2):
                rows = slice((2 * i + j) * shards, (2 * i + j + 1) * shards)
                pairs.append((spec[rows, :width], spec[rows, width:]))
            part = signals_from(pairs, shards, width, cos, sin, last_ref)
            for j in range(2):
                ys[pl.ds(j * channels + c, shards, stride=both), :] = part[:, j * width : (j + 1) * width]
                for p in range(2):
                    column = jnp.broadcast_to(part[:, j * width + p : j * width + p + 1], (shards, width))
                    firsts[2 * j + p] = jnp.where(lane_channel == c, column, firsts[2 * j + p])
        for k in range(4):
            first_s[k, :shards, :] += firsts[k]

    out_ref[:, :both, :] = ys[...].astype(BF16).reshape(shards, both, width)
    extra_s[...] = jnp.zeros_like(extra_s)
    for k in range(4):
        extra_s[pl.ds(k, shards, stride=8), :] = first_s[k, 1 : shards + 1, :]
    out_ref[:, both:, :] = extra_s[...].astype(BF16).reshape(shards, 8, width)


def post_kernel(r_ref, g_ref, qs_ref, ks_ref, vs_ref, ends_ref, next_ref, taps_ref, mixed_ref, q_ref, k_ref, v_ref, ext, around):
    rows, channels = g_ref.shape
    group = (r_ref.shape[1] - 8) // 2
    count = 128 // group
    shape = (count, 8, 128)
    mine = lax.broadcasted_iota(jnp.int32, shape, 2) // group == lax.broadcasted_iota(jnp.int32, shape, 0)
    for lane in range(0, channels, 128):
        lanes = pl.ds(lane, 128)
        blocks = pl.ds(lane // group, count)
        mix = r_ref[blocks, :group, :].reshape(128, rows).astype(F32).T
        back = r_ref[blocks, group : 2 * group, :].reshape(128, rows).astype(F32).T
        beyond = jnp.sum(jnp.where(mine, r_ref[blocks, 2 * group :, :].astype(F32), 0.0), 0)
        mixed_ref[:, lanes] = (qs_ref[:, lanes].astype(F32) * mix).astype(BF16)
        near = (g_ref, ks_ref, vs_ref)
        gate, key, value = [ref[:, lanes].astype(F32) for ref in near]
        gate_next = next_ref[0, :, lanes].astype(F32)
        shorts_next = []
        for p in (1, 2):
            around[0:2, :] = ends_ref[p - 1, :, lanes].astype(F32)
            around[2:4, :] = next_ref[p, :, lanes].astype(F32)
            shorts_next.append(
                (
                    taps_ref[p, 0:1, lanes] * around[2:4, :]
                    + taps_ref[p, 1:2, lanes] * around[1:3, :]
                    + taps_ref[p, 2:3, lanes] * around[0:2, :]
                )
                .astype(BF16)
                .astype(F32)
            )
        key_next, value_next = shorts_next
        parts = (gate * mix, back * value, back * key)
        beyonds = (gate_next * beyond[0:2], beyond[2:4] * value_next, beyond[2:4] * key_next)
        for p, ref in enumerate((q_ref, k_ref, v_ref)):
            ext[p, 0:rows, :] = parts[p]
            ext[p, rows : rows + 2, :] = beyonds[p]
            ref[:, lanes] = (
                taps_ref[p, 0:1, lanes] * parts[p]
                + taps_ref[p, 1:2, lanes] * ext[p, 1 : rows + 1, :]
                + taps_ref[p, 2:3, lanes] * ext[p, 2 : rows + 2, :]
            ).astype(BF16)


def add_kernel(near_ref, far_ref, out_ref):
    out_ref[...] = near_ref[...] + far_ref[...].astype(F32)


def per_device(query_proj, key_proj, value_proj, short_taps, skip_gain, long_filter, out_grad):
    positions, width = query_proj.shape
    channels, length = long_filter.shape
    shards = lax.axis_size("seq")
    table, twist = make_tables(shards, positions)
    shape = jax.ShapeDtypeStruct

    near = [pltpu.with_memory_space_constraint(x, pltpu.HBM) for x in (query_proj, key_proj, value_proj, out_grad)]
    ends, starts = call(
        ends_kernel,
        (shape((3, 2, width), BF16), shape((3, 2, width), BF16)),
        [pltpu.VMEM((6, 16, width), BF16), pltpu.SemaphoreType.DMA((6,))],
        bytes_accessed=200 * width,
        in_specs=[pl.BlockSpec(memory_space=pltpu.HBM)] * 4,
    )(*near)
    previous = passed_along(ends, "seq", 1)
    previous, filter_sent = lax.optimization_barrier((previous, long_filter.astype(BF16)))
    filter_far = to_mirror(filter_sent)
    wide = shape((positions, width), BF16)
    query_short, key_short, value_short, send, own_ends = call(
        pre_kernel,
        (wide, wide, wide, shape((shards, 2 * channels, positions), BF16), shape((2, 2, width), BF16)),
        [
            *[pltpu.VMEM((positions, width), BF16)] * 4,
            pltpu.VMEM((3, positions + 8, 128), F32),
            pltpu.SemaphoreType.DMA((4,)),
        ],
        flops=30 * positions * width,
        bytes_accessed=18 * positions * width,
        in_specs=[pl.BlockSpec(memory_space=pltpu.HBM)] * 4
        + [pl.BlockSpec(memory_space=pltpu.VMEM)] * 2,
    )(*near, previous, short_taps)
    received = lax.all_to_all(send, "seq", split_axis=0, concat_axis=0, tiled=True)

    step = 4
    spectrum = call(
        spectrum_kernel,
        shape((channels * shards, 2 * positions), F32),
        [
            pltpu.VMEM((shards * channels, positions), F32),
            pltpu.VMEM((shards * channels, positions), F32),
            pltpu.VMEM((step * shards, 4 * positions), BF16),
        ],
        flops=SPEC_FLOPS,
        bytes_accessed=14 * channels * length,
        in_specs=[pl.BlockSpec(memory_space=pltpu.VMEM)] * 2
        + [pl.BlockSpec(memory_space=pltpu.SMEM)]
        + [pl.BlockSpec(memory_space=pltpu.VMEM)] * 2,
    )(long_filter, filter_far, skip_gain, table, twist)

    received, spectrum = lax.optimization_barrier((received, spectrum))
    spectra, lagged, lagged_back = call(
        corr_kernel,
        (
            shape((2 * channels * shards, 2 * positions), F32),
            shape((channels, length), F32),
            shape((channels, length), BF16),
        ),
        [
            pltpu.VMEM((shards * 2 * channels, positions), F32),
            pltpu.VMEM((shards * channels, positions), F32),
            pltpu.VMEM((shards * channels, positions), F32),
            pltpu.VMEM((2 * step * shards, 2 * positions), BF16),
            pltpu.VMEM((step * shards, 4 * positions), F32),
        ],
        flops=CORR_FLOPS,
        bytes_accessed=24 * channels * length,
    )(received, table, twist)
    lagged_far = to_mirror(lagged_back)

    returned = call(
        mix_kernel,
        shape((shards, 2 * channels + 8, positions), BF16),
        [
            pltpu.VMEM((shards * 2 * channels, positions), F32),
            pltpu.VMEM((2 * step * shards, 2 * positions), BF16),
            pltpu.VMEM((2 * step * shards, 2 * positions), F32),
            pltpu.VMEM((4, shards + 8, positions), F32),
            pltpu.VMEM((shards * 8, positions), F32),
        ],
        flops=MIX_FLOPS,
        bytes_accessed=24 * channels * length,
    )(spectra, spectrum, table, twist)
    result = lax.all_to_all(returned, "seq", split_axis=0, concat_axis=0, tiled=True)

    filter_grad = call(
        add_kernel,
        shape((channels, length), F32),
        flops=ADD_FLOPS,
        bytes_accessed=10 * channels * length,
    )(lagged, lagged_far)
    starts, filter_grad = lax.optimization_barrier((starts, filter_grad))
    following = passed_along(starts, "seq", -1)
    mixed_out, query_grad, key_grad, value_grad = call(
        post_kernel,
        (wide, wide, wide, wide),
        [pltpu.VMEM((3, positions + 8, 128), F32), pltpu.VMEM((8, 128), F32)],
        flops=30 * positions * width,
        bytes_accessed=20 * positions * width,
    )(result, out_grad, query_short, key_short, value_short, own_ends, following, short_taps)
    return (mixed_out, query_grad, key_grad, value_grad, filter_grad)


def solution(mesh):
    in_specs = (
        P("seq", "chan"),
        P("seq", "chan"),
        P("seq", "chan"),
        P(None, None, "chan"),
        P("chan"),
        P(("chan", "seq"), None),
        P("seq", "chan"),
    )
    out_specs = (
        P("seq", "chan"),
        P("seq", "chan"),
        P("seq", "chan"),
        P("seq", "chan"),
        P(("chan", "seq"), None),
    )
    return jax.shard_map(
        per_device, mesh=mesh, in_specs=in_specs, out_specs=out_specs, check_vma=False
    )
```

time: 108 us -> 88.1 us (0.82)
  starting transfers between devices: 40.6 us -> 33 us
  local copies, waits for them, and re-layouts: 10.6 us -> 3.27 us
  waiting for transfers between devices: 39.8 us -> 33.5 us
  Pallas kernels: 14 us -> 16 us
    ppermute x2, waiting for transfers between devices: 28.3 us -> 11.4 us  [to_mirror(): lax.ppermute(array, ('seq', 'chan'), [(i, count - 1 - i) for i in range(c...]
    all_to_all x1, waiting for transfers between devices: 0.01 us -> 9.6 us  [per_device(): lax.all_to_all(send, 'seq', split_axis=0, concat_axis=0, tiled=True)]
    all_to_all x1, starting transfers between devices: 14.2 us -> 5.61 us  [per_device(): lax.all_to_all(send, 'seq', split_axis=0, concat_axis=0, tiled=True)]
    ppermute x2, waiting for transfers between devices: 0.82 us -> 7.4 us  [passed_along(): return lax.ppermute(array, axis, pairs)]
    all_to_all x1, waiting for transfers between devices: 10.7 us -> 5.04 us  [per_device(): lax.all_to_all(returned, 'seq', split_axis=0, concat_axis=0, tiled=True)]
    unnamed x32 -> x22, local copies, waits for them, and re-layouts: 7.89 us -> 3.27 us
    all_to_all x1, starting transfers between devices: 5.56 us -> 7.23 us  [per_device(): lax.all_to_all(returned, 'seq', split_axis=0, concat_axis=0, tiled=True)]
    another operation x2 -> x0, local copies, waits for them, and re-layouts: 1.47 us -> none  [per_device(): jnp.stack([x[positions - 2:] for x in (query_proj, key_proj, value_proj)])]
  transfers between devices with their start and end apart: 6 -> 6, of which waited for: 4 -> 5; matrix products, arithmetic and copies ran while one was open for 2% -> 1% of each run, Pallas kernels for 5% -> 11%
where the time goes in v1:
time: 88.1 us; the launch traced here: 87.7 us
  waiting for transfers between devices  33.5 us (38%)
  starting transfers between devices  33 us (37%)
  Pallas kernels  16 us (18%)
  local copies, waits for them, and re-layouts  3.27 us (4%)
  other arithmetic  1.07 us (1%)
    ppermute x2, starting transfers between devices, to_mirror(): lax.ppermute(array, ('seq', 'chan'), [(i, count - 1 - i) for i in range(c...  14.5 us
    ppermute x2, waiting for transfers between devices, to_mirror(): lax.ppermute(array, ('seq', 'chan'), [(i, count - 1 - i) for i in range(c...  11.4 us
    all_to_all x1, waiting for transfers between devices, per_device(): lax.all_to_all(send, 'seq', split_axis=0, concat_axis=0, tiled=True)  9.6 us
    ppermute x2, waiting for transfers between devices, passed_along(): return lax.ppermute(array, axis, pairs)  7.4 us
    all_to_all x1, starting transfers between devices, per_device(): lax.all_to_all(returned, 'seq', split_axis=0, concat_axis=0, tiled=True)  7.23 us
    ppermute x2, starting transfers between devices, passed_along(): return lax.ppermute(array, axis, pairs)  5.65 us
    all_to_all x1, starting transfers between devices, per_device(): lax.all_to_all(send, 'seq', split_axis=0, concat_axis=0, tiled=True)  5.61 us
    all_to_all x1, waiting for transfers between devices, per_device(): lax.all_to_all(returned, 'seq', split_axis=0, concat_axis=0, tiled=True)  5.04 us
  transfers between devices with their start and end apart: 6, of which 5 were waited for; matrix products, arithmetic and copies ran while one was open for 1% of the time, Pallas kernels for 11%

profile of v1, /device:TPU:1, one launch (start us, length us, event | category | flops | bytes accessed | tf_op | source)
XLA Modules:
  0.0 87.7 jit_solution(702620557131475857)
XLA Ops:
  0.6 0.0 copy-start.2
  0.6 0.0 copy-start.5
  0.7 0.0 copy-start.1
  0.7 0.0 copy-start.8
  0.7 1.0 %shard_map.128 = (bf16[3,2,1024]{2,1,0:T(2,128)(2,1)S(1)}, bf16[3,2,1024]{2,1,0:T(2,128)(2,1)S(1)}) custom-call(bf16[128,1024]{1,0:T(8,128)(2,1)} %q_hbm.3, bf16[128,1024]{1,0:T(8,128)(2,1)} %k_hbm.3, bf16[128,1024]{1,0:T(8,128)(2,1)} %v_hbm.3, bf16[128,1024]{1,0:T(8,128)(2,1)} %g_ref.1), custom_call_target="tpu_custom_call" | custom-call | bytes 204800 | tf_op jit(solution)/shard_map/pallas_call | solution.py:349
  1.7 4.4 %collective-permute-start = (bf16[3,2,1024]{2,1,0:T(2,128)(2,1)S(1)}, bf16[3,2,1024]{2,1,0:T(2,128)(2,1)S(1)}, u32[]{:S(2)}, u32[]{:S(2)}) collective-permute-start(bf16[3,2,1024]{2,1,0:T(2,128)(2,1)S(1)} %get-tuple-element.25), channel_id=1, source_target_pairs={{0,4},{4,8},{8,12},{12,16},{16,20},{20,24},{24,28},{28,32},{32,36}... | collective-permute-start | bytes 36872 | tf_op jit(solution)/shard_map/ppermute | solution.py:24
  6.0 1.1 %convert_element_type.3 = bf16[16,8192]{1,0:T(8,128)(2,1)S(1)} convert(f32[16,8192]{1,0:T(8,128)} %own_ref.1) | non-fusion elementwise | flops 131072 | bytes 786432 | tf_op jit(solution)/shard_map/convert_element_type | solution.py:357
  7.1 0.0 collective-permute-done.halo_ref
  7.1 11.7 %collective-permute-start.1 = (bf16[16,8192]{1,0:T(8,128)(2,1)S(1)}, bf16[16,8192]{1,0:T(8,128)(2,1)S(1)}, u32[]{:S(2)}, u32[]{:S(2)}) collective-permute-start(bf16[16,8192]{1,0:T(8,128)(2,1)S(1)} %convert_element_type.3), channel_id=1, source_target_pairs={{0,255},{1,254},{2,253},{3,252},{4,251},{5,250},{6,249},{7,248},{8... | collective-permute-start | bytes 786440 | tf_op jit(solution)/shard_map/ppermute | solution.py:29
  18.9 0.0 copy-start.3
  18.9 0.8 copy-done.3
  19.7 2.8 %shard_map.129 = (bf16[128,1024]{1,0:T(8,128)(2,1)S(1)}, bf16[128,1024]{1,0:T(8,128)(2,1)S(1)}, bf16[128,1024]{1,0:T(8,128)(2,1)S(1)}, bf16[64,32,128]{2,1,0:T(8,128)(2,1)}, bf16[2,2,1024]{2,1,0:T(2,128)(2,1)S(1)}) custom-call(bf16[128,1024]{1,0:T(8,128)(2,1)} %q_hbm.3, bf16[128,1024]{1,0:T(8,128)(2,1)} %k_hbm.3, bf16[128,1024]{1,0:T(8,128)(2,1)} %v_hbm.3, ...), custom_call_target="tpu_custom_call" | custom-call | flops 3932160 | bytes 2359296 | tf_op jit(solution)/shard_map/pallas_call | solution.py:360
  22.5 5.6 %all-to-all-start = ((bf16[64,32,128]{2,1,0:T(8,128)(2,1)}), bf16[64,32,128]{2,1,0:T(8,128)(2,1)S(1)}, u32[]{:S(2)}, u32[]{:S(2)}) async-start(bf16[64,32,128]{2,1,0:T(8,128)(2,1)} %get-tuple-element.27), calls=%async_computation | async-start | bytes 1048576 | tf_op jit(solution)/shard_map/all_to_all | solution.py:373
  28.1 4.6 %collective-permute-done.1.mir_ref = bf16[16,8192]{1,0:T(8,128)(2,1)S(1)} collective-permute-done((bf16[16,8192]{1,0:T(8,128)(2,1)S(1)}, bf16[16,8192]{1,0:T(8,128)(2,1)S(1)}, u32[]{:S(2)}, u32[]{:S(2)}) %collective-permute-start.1) | collective-permute-done | bytes 262176 | tf_op jit(solution)/shard_map/ppermute | solution.py:29
  32.7 0.0 copy-start.6
  32.7 0.7 copy-done.6
  33.4 0.0 copy-done.2
  33.4 0.0 copy-done.5
  33.4 0.0 copy-done.1
  33.4 0.0 copy-done.8
  33.4 0.0 copy-start.7
  33.5 0.9 %copy-done.7 = bf16[16,8192]{1,0:T(8,128)(2,1)S(1)} copy-done((bf16[16,8192]{1,0:T(8,128)(2,1)S(1)}, bf16[16,8192]{1,0:T(8,128)(2,1)}, u32[]{:S(2)}) %copy-start.7) | copy-done | bytes 262168
  34.4 2.6 %shard_map.130.spec_ref = f32[1024,256]{1,0:T(8,128)S(1)} custom-call(f32[16,8192]{1,0:T(8,128)S(1)} %copy-done.1, bf16[16,8192]{1,0:T(8,128)(2,1)S(1)} %copy-done.7, f32[1024]{0:T(1024)S(1)} %copy-done.8, bf16[960,256]{1,0:T(8,128)(2,1)S(1)} %copy-done.2, f32[2,64,128]{2,1,0:T(8,128)S(1)} %copy-done.5), custom_call_target="tpu_custom_call" | custom-call | flops 17179869184 | bytes 1835008 | tf_op jit(solution)/shard_map/pallas_call | solution.py:376
  37.0 9.6 %all-to-all-done.x_ref = bf16[64,32,128]{2,1,0:T(8,128)(2,1)S(1)} async-done(((bf16[64,32,128]{2,1,0:T(8,128)(2,1)}), bf16[64,32,128]{2,1,0:T(8,128)(2,1)S(1)}, u32[]{:S(2)}, u32[]{:S(2)}) %all-to-all-start) | async-done | bytes 524320 | tf_op jit(solution)/shard_map/all_to_all | solution.py:373
  46.6 3.5 %shard_map.131 = (f32[2048,256]{1,0:T(8,128)S(1)}, f32[16,8192]{1,0:T(8,128)S(1)}, bf16[16,8192]{1,0:T(8,128)(2,1)S(1)}) custom-call(bf16[64,32,128]{2,1,0:T(8,128)(2,1)S(1)} %all-to-all-done.x_ref, bf16[960,256]{1,0:T(8,128)(2,1)S(1)} %copy-done.2, f32[2,64,128]{2,1,0:T(8,128)S(1)} %copy-done.5), custom_call_target="tpu_custom_call" | custom-call | flops 536870912 | bytes 3145728 | tf_op jit(solution)/shard_map/pallas_call | solution.py:392
  50.1 0.0 copy-start.9
  50.2 0.8 copy-done.9
  50.9 2.8 %collective-permute-start.2 = (bf16[16,8192]{1,0:T(8,128)(2,1)S(1)}, bf16[16,8192]{1,0:T(8,128)(2,1)S(1)}, u32[]{:S(2)}, u32[]{:S(2)}) collective-permute-start(bf16[16,8192]{1,0:T(8,128)(2,1)S(1)} %get-tuple-element.38), channel_id=1, source_target_pairs={{0,255},{1,254},{2,253},{3,252},{4,251},{5,250},{6,249},{7,248},{8... | collective-permute-start | bytes 786440 | tf_op jit(solution)/shard_map/ppermute | solution.py:29
  53.7 0.0 copy-start.10
  53.7 3.5 %shard_map.132 = bf16[64,40,128]{2,1,0:T(8,128)(2,1)} custom-call(f32[2048,256]{1,0:T(8,128)S(1)} %get-tuple-element.30.spectra_ref, f32[1024,256]{1,0:T(8,128)S(1)} %shard_map.130.spec_ref, bf16[960,256]{1,0:T(8,128)(2,1)S(1)} %copy-done.2, f32[2,64,128]{2,1,0:T(8,128)S(1)} %copy-done.5), custom_call_target="tpu_custom_call" | custom-call | flops 536870912 | bytes 3145728 | tf_op jit(solution)/shard_map/pallas_call | solution.py:411
  57.3 7.2 %all-to-all-start.1 = ((bf16[64,40,128]{2,1,0:T(8,128)(2,1)}), bf16[64,40,128]{2,1,0:T(8,128)(2,1)S(1)}, u32[]{:S(2)}, u32[]{:S(2)}) async-start(bf16[64,40,128]{2,1,0:T(8,128)(2,1)} %shard_map.132), calls=%async_computation.1 | async-start | bytes 1310720 | tf_op jit(solution)/shard_map/all_to_all | solution.py:424
  64.5 6.8 %collective-permute-done.2.far_ref = bf16[16,8192]{1,0:T(8,128)(2,1)S(1)} collective-permute-done((bf16[16,8192]{1,0:T(8,128)(2,1)S(1)}, bf16[16,8192]{1,0:T(8,128)(2,1)S(1)}, u32[]{:S(2)}, u32[]{:S(2)}) %collective-permute-start.2) | collective-permute-done | bytes 262176 | tf_op jit(solution)/shard_map/ppermute | solution.py:29
  71.3 0.0 copy-done.10
  71.3 0.0 copy-start
  71.3 0.0 copy-start.4
  71.3 0.8 shard_map.133
  72.2 1.3 %collective-permute-start.3 = (bf16[3,2,1024]{2,1,0:T(2,128)(2,1)S(1)}, bf16[3,2,1024]{2,1,0:T(2,128)(2,1)S(1)}, u32[]{:S(2)}, u32[]{:S(2)}) collective-permute-start(bf16[3,2,1024]{2,1,0:T(2,128)(2,1)S(1)} %get-tuple-element.39), channel_id=1, source_target_pairs={{4,0},{8,4},{12,8},{16,12},{20,16},{24,20},{28,24},{32,28},{36,32}... | collective-permute-start | bytes 36872 | tf_op jit(solution)/shard_map/ppermute | solution.py:24
  73.5 7.4 %collective-permute-done.3.next_ref = bf16[3,2,1024]{2,1,0:T(2,128)(2,1)S(1)} collective-permute-done((bf16[3,2,1024]{2,1,0:T(2,128)(2,1)S(1)}, bf16[3,2,1024]{2,1,0:T(2,128)(2,1)S(1)}, u32[]{:S(2)}, u32[]{:S(2)}) %collective-permute-start.3) | collective-permute-done | bytes 12320 | tf_op jit(solution)/shard_map/ppermute | solution.py:24
  80.9 5.0 %all-to-all-done.1.r_ref = bf16[64,40,128]{2,1,0:T(8,128)(2,1)S(1)} async-done(((bf16[64,40,128]{2,1,0:T(8,128)(2,1)}), bf16[64,40,128]{2,1,0:T(8,128)(2,1)S(1)}, u32[]{:S(2)}, u32[]{:S(2)}) %all-to-all-start.1) | async-done | bytes 655392 | tf_op jit(solution)/shard_map/all_to_all | solution.py:424
  85.9 0.0 copy-done
  85.9 0.0 copy-done.4
  85.9 1.8 %shard_map.134 = (bf16[128,1024]{1,0:T(8,128)(2,1)}, bf16[128,1024]{1,0:T(8,128)(2,1)}, bf16[128,1024]{1,0:T(8,128)(2,1)}, bf16[128,1024]{1,0:T(8,128)(2,1)}) custom-call(bf16[64,40,128]{2,1,0:T(8,128)(2,1)S(1)} %all-to-all-done.1.r_ref, bf16[128,1024]{1,0:T(8,128)(2,1)S(1)} %copy-done, bf16[128,1024]{1,0:T(8,128)(2,1)S(1)} %get-tuple-element.32.qs_ref, ...), custom_call_target="tpu_custom_call" | custom-call | flops 3932160 | bytes 2621440 | tf_op jit(solution)/shard_map/pallas_call | solution.py:434
Async XLA Ops:
  0.6 32.8 %copy-start.2 = (bf16[960,256]{1,0:T(8,128)(2,1)S(1)}, bf16[960,256]{1,0:T(8,128)(2,1)}, u32[]{:S(2)}) copy-start(bf16[960,256]{1,0:T(8,128)(2,1)} %constant.4.clone.table_ref) | copy-start | bytes 1474564
  0.6 32.8 %copy-start.5 = (f32[2,64,128]{2,1,0:T(8,128)S(1)}, f32[2,64,128]{2,1,0:T(8,128)}, u32[]{:S(2)}) copy-start(f32[2,64,128]{2,1,0:T(8,128)} %constant.5.clone.twist_ref) | copy-start | bytes 196612
  0.7 32.8 %copy-start.1 = (f32[16,8192]{1,0:T(8,128)S(1)}, f32[16,8192]{1,0:T(8,128)}, u32[]{:S(2)}) copy-start(f32[16,8192]{1,0:T(8,128)} %own_ref.1) | copy-start | bytes 1572868
  0.7 32.8 %copy-start.8 = (f32[1024]{0:T(1024)S(1)}, f32[1024]{0:T(1024)}, u32[]{:S(2)}) copy-start(f32[1024]{0:T(1024)} %skip_ref.1) | copy-start | bytes 12292
  1.7 5.5 %collective-permute-start = (bf16[3,2,1024]{2,1,0:T(2,128)(2,1)S(1)}, bf16[3,2,1024]{2,1,0:T(2,128)(2,1)S(1)}, u32[]{:S(2)}, u32[]{:S(2)}) collective-permute-start(bf16[3,2,1024]{2,1,0:T(2,128)(2,1)S(1)} %get-tuple-element.25), channel_id=1, source_target_pairs={{0,4},{4,8},{8,12},{12,16},{16,20},{20,24},{24,28},{28,32},{32,36}... | collective-permute-start | bytes 36872 | tf_op jit(solution)/shard_map/ppermute | solution.py:24
  7.1 25.6 %collective-permute-start.1 = (bf16[16,8192]{1,0:T(8,128)(2,1)S(1)}, bf16[16,8192]{1,0:T(8,128)(2,1)S(1)}, u32[]{:S(2)}, u32[]{:S(2)}) collective-permute-start(bf16[16,8192]{1,0:T(8,128)(2,1)S(1)} %convert_element_type.3), channel_id=1, source_target_pairs={{0,255},{1,254},{2,253},{3,252},{4,251},{5,250},{6,249},{7,248},{8... | collective-permute-start | bytes 786440 | tf_op jit(solution)/shard_map/ppermute | solution.py:29
  18.9 0.8 copy-start.3
  22.5 24.1 %all-to-all-start = ((bf16[64,32,128]{2,1,0:T(8,128)(2,1)}), bf16[64,32,128]{2,1,0:T(8,128)(2,1)S(1)}, u32[]{:S(2)}, u32[]{:S(2)}) async-start(bf16[64,32,128]{2,1,0:T(8,128)(2,1)} %get-tuple-element.27), calls=%async_computation | async-start | bytes 1048576 | tf_op jit(solution)/shard_map/all_to_all | solution.py:373
  32.7 0.7 copy-start.6
  33.4 1.0 %copy-start.7 = (bf16[16,8192]{1,0:T(8,128)(2,1)S(1)}, bf16[16,8192]{1,0:T(8,128)(2,1)}, u32[]{:S(2)}) copy-start(bf16[16,8192]{1,0:T(8,128)(2,1)} %copy-done.6) | copy-start | bytes 786436
  50.1 0.8 copy-start.9
  50.9 20.4 %collective-permute-start.2 = (bf16[16,8192]{1,0:T(8,128)(2,1)S(1)}, bf16[16,8192]{1,0:T(8,128)(2,1)S(1)}, u32[]{:S(2)}, u32[]{:S(2)}) collective-permute-start(bf16[16,8192]{1,0:T(8,128)(2,1)S(1)} %get-tuple-element.38), channel_id=1, source_target_pairs={{0,255},{1,254},{2,253},{3,252},{4,251},{5,250},{6,249},{7,248},{8... | collective-permute-start | bytes 786440 | tf_op jit(solution)/shard_map/ppermute | solution.py:29
  53.7 17.6 %copy-start.10 = (f32[16,8192]{1,0:T(8,128)S(1)}, f32[16,8192]{1,0:T(8,128)}, u32[]{:S(2)}) copy-start(f32[16,8192]{1,0:T(8,128)} %copy-done.9) | copy-start | bytes 1572868
  57.3 28.6 %all-to-all-start.1 = ((bf16[64,40,128]{2,1,0:T(8,128)(2,1)}), bf16[64,40,128]{2,1,0:T(8,128)(2,1)S(1)}, u32[]{:S(2)}, u32[]{:S(2)}) async-start(bf16[64,40,128]{2,1,0:T(8,128)(2,1)} %shard_map.132), calls=%async_computation.1 | async-start | bytes 1310720 | tf_op jit(solution)/shard_map/all_to_all | solution.py:424
  71.3 14.6 %copy-start = (bf16[128,1024]{1,0:T(8,128)(2,1)S(1)}, bf16[128,1024]{1,0:T(8,128)(2,1)}, u32[]{:S(2)}) copy-start(bf16[128,1024]{1,0:T(8,128)(2,1)} %g_ref.1) | copy-start | bytes 786436
  71.3 14.6 %copy-start.4 = (f32[3,3,1024]{2,1,0:T(4,128)S(1)}, f32[3,3,1024]{2,1,0:T(4,128)}, u32[]{:S(2)}) copy-start(f32[3,3,1024]{2,1,0:T(4,128)} %taps_ref.3) | copy-start | bytes 110596
  72.2 8.7 %collective-permute-start.3 = (bf16[3,2,1024]{2,1,0:T(2,128)(2,1)S(1)}, bf16[3,2,1024]{2,1,0:T(2,128)(2,1)S(1)}, u32[]{:S(2)}, u32[]{:S(2)}) collective-permute-start(bf16[3,2,1024]{2,1,0:T(2,128)(2,1)S(1)} %get-tuple-element.39), channel_id=1, source_target_pairs={{4,0},{8,4},{12,8},{16,12},{20,16},{24,20},{28,24},{32,28},{36,32}... | collective-permute-start | bytes 36872 | tf_op jit(solution)/shard_map/ppermute | solution.py:24

commit v2 on v1

--- a/solution.py
+++ b/solution.py
@@ -45,7 +45,7 @@
     first_thrice = np.concatenate([high, low, high], 1)
     last = first.T / (shards * width)
     high, low = split_bf16(last)
-    last_twice = np.concatenate([high, low], 1)
+    last_twice = np.pad(np.concatenate([high, low], 0), ((0, 0), (0, 2 * width - 2 * shards)))
     twist = 2.0 * np.pi * k1.T * n2[None, :] / (2 * shards * width)
     twist = np.stack([np.cos(twist), np.sin(twist)]).astype(np.float32)
     inner = 2.0 * np.pi * (n2[:, None] * n2[None, :] % width) / width
@@ -67,7 +67,7 @@
         back=table_ref.at[4 * width : at],
         first_twice=table_ref.at[at : at + 2 * shards, : 2 * shards],
         first_thrice=table_ref.at[at : at + 2 * shards, : 3 * shards],
-        last_twice=table_ref.at[at + 2 * shards : at + 3 * shards, :],
+        last_twice=table_ref.at[at + 2 * shards : at + 4 * shards, : 2 * shards],
     )
 
 
@@ -102,41 +102,58 @@
             first_ref[p - 3] = held[p].astype(F32)[0:2].astype(BF16)
 
 
-def pre_kernel(q_hbm, k_hbm, v_hbm, g_hbm, halo_ref, taps_ref, qs_ref, ks_ref, vs_ref, send_ref, ends_ref, q_ref, k_ref, v_ref, g_ref, ext, sems):
-    copies = [
-        pltpu.make_async_copy(src, dst, sems.at[p])
-        for p, (src, dst) in enumerate(((q_hbm, q_ref), (k_hbm, k_ref), (v_hbm, v_ref), (g_hbm, g_ref)))
-    ]
-    for copy in copies:
-        copy.start()
-    for copy in copies:
-        copy.wait()
+def pre_kernel(
+    q_hbm, k_hbm, v_hbm, g_hbm, taps_hbm, halo_ref, qs_ref, ks_ref, vs_ref, send_hbm, ends_ref, q_ref, k_ref, v_ref, g_ref, taps_ref, send_ref, ext, sems, out_sems
+):
     rows, channels = q_ref.shape
     group = send_ref.shape[1] // 2
-    for lane in range(0, channels, 128):
-        lanes = pl.ds(lane, 128)
-        shorts = []
-        for p, ref in enumerate((q_ref, k_ref, v_ref)):
-            ext[p, 6:8, :] = halo_ref[p, :, lanes].astype(F32)
-            ext[p, 8 : rows + 8, :] = ref[:, lanes].astype(F32)
-            shorts.append(
-                (
-                    taps_ref[p, 0:1, lanes] * ext[p, 8 : rows + 8, :]
-                    + taps_ref[p, 1:2, lanes] * ext[p, 7 : rows + 7, :]
-                    + taps_ref[p, 2:3, lanes] * ext[p, 6 : rows + 6, :]
-                ).astype(BF16)
-            )
-        qs, ks, vs = shorts
-        qs_ref[:, lanes] = qs
-        ks_ref[:, lanes] = ks
-        vs_ref[:, lanes] = vs
-        product = ks.astype(F32) * vs.astype(F32)
-        gate = g_ref[:, lanes].astype(F32) * qs.astype(F32)
-        for p in (1, 2):
-            ends_ref[p - 1, :, lanes] = ext[p, rows + 6 : rows + 8, :].astype(BF16)
-        blocks = pl.ds(lane // group, 128 // group)
-        send_ref[blocks, 0:group, :] = product.T.astype(BF16).reshape(128 // group, group, rows)
-        send_ref[blocks, group:, :] = gate.T.astype(BF16).reshape(128 // group, group, rows)
+    chunks = sems.shape[0]
+    size = channels // chunks
+    taps_copy = pltpu.make_async_copy(taps_hbm, taps_ref, out_sems.at[chunks])
+    taps_copy.start()
+    pairs = ((q_hbm, q_ref), (k_hbm, k_ref), (v_hbm, v_ref), (g_hbm, g_ref))
+    copies = []
+    for chunk in range(chunks):
+        lanes = pl.ds(chunk * size, size)
+        copies.append(
+            [pltpu.make_async_copy(src.at[:, lanes], dst.at[:, lanes], sems.at[chunk, p]) for p, (src, dst) in enumerate(pairs)]
+        )
+        for copy in copies[-1]:
+            copy.start()
+    taps_copy.wait()
+    sends = []
+    for chunk in range(chunks):
+        for copy in copies[chunk]:
+            copy.wait()
+        for lane in range(chunk * size, (chunk + 1) * size, 128):
+            lanes = pl.ds(lane, 128)
+            shorts = []
+            for p, ref in enumerate((q_ref, k_ref, v_ref)):
+                ext[p, 6:8, :] = halo_ref[p, :, lanes].astype(F32)
+                ext[p, 8 : rows + 8, :] = ref[:, lanes].astype(F32)
+                shorts.append(
+                    (
+                        taps_ref[p, 0:1, lanes] * ext[p, 8 : rows + 8, :]
+                        + taps_ref[p, 1:2, lanes] * ext[p, 7 : rows + 7, :]
+                        + taps_ref[p, 2:3, lanes] * ext[p, 6 : rows + 6, :]
+                    ).astype(BF16)
+                )
+            qs, ks, vs = shorts
+            qs_ref[:, lanes] = qs
+            ks_ref[:, lanes] = ks
+            vs_ref[:, lanes] = vs
+            product = ks.astype(F32) * vs.astype(F32)
+            gate = g_ref[:, lanes].astype(F32) * qs.astype(F32)
+            for p in (1, 2):
+                ends_ref[p - 1, :, lanes] = ext[p, rows + 6 : rows + 8, :].astype(BF16)
+            blocks = pl.ds(lane // group, 128 // group)
+            send_ref[blocks, 0:group, :] = product.T.astype(BF16).reshape(128 // group, group, rows)
+            send_ref[blocks, group:, :] = gate.T.astype(BF16).reshape(128 // group, group, rows)
+        blocks = pl.ds(chunk * size // group, size // group)
+        sends.append(pltpu.make_async_copy(send_ref.at[blocks], send_hbm.at[blocks], out_sems.at[chunk]))
+        sends[-1].start()
+    for copy in sends:
+        copy.wait()
 
 
 def spectrum_kernel(own_ref, mir_ref, skip_ref, table_ref, twist_ref, out_ref, own_s, mir_s, lhs):
@@ -184,11 +201,11 @@
         columns.append(
             jnp.concatenate([(real * cos - imag * sin).astype(BF16), (imag * cos + real * sin).astype(BF16)], 0)
         )
-    rhs = jnp.concatenate(columns, 1)
-    return dot(last_ref[...], jnp.concatenate([rhs, rhs], 0))
-
-
-def corr_kernel(x_ref, table_ref, twist_ref, spectra_ref, own_ref, mir_ref, xs, own_s, mir_s, lhs, spec):
+    parts = dot(last_ref[...], columns[0] if len(columns) == 1 else jnp.concatenate(columns, 1))
+    return parts[:shards] + parts[shards:]
+
+
+def corr_kernel(x_ref, table_ref, twist_ref, spectra_ref, corr_ref, mir_ref, xs, mir_s, lhs, spec):
     shards, both, width = x_ref.shape
     channels = both // 2
     table = table_views(table_ref, shards, width)
@@ -196,7 +213,7 @@
     scale = 1.0 / math.sqrt(shards * width)
     xs[...] = x_ref[...].reshape(shards * both, width).astype(F32)
     cos, sin = twist_ref[0], twist_ref[1]
-    step = 4
+    step = 8
 
     @pl.loop(0, channels, step=step)
     def _(base):
@@ -219,25 +236,21 @@
             pi = both_spec[2 * i * shards : (2 * i + 1) * shards, width:]
             gr = both_spec[(2 * i + 1) * shards : (2 * i + 2) * shards, :width]
             gi = both_spec[(2 * i + 1) * shards : (2 * i + 2) * shards, width:]
-            rows = pl.ds(i * shards, shards)
-            lhs[rows, :width] = (pr * gr + pi * gi).astype(BF16)
-            lhs[rows, width:] = (pr * gi - pi * gr).astype(BF16)
-        product = lhs[: step * shards, :]
-        spec[:, : 2 * width] = dot(product, table["back"][...])
-        spec[:, 2 * width :] = dot(product, table["conj"][...])
-        for i in range(step):
-            c = base + i
-            rows = slice(i * shards, (i + 1) * shards)
+            rows = pl.ds((base + i) * shards, shards)
+            corr_ref[rows, :width] = (pr * gr + pi * gi).astype(BF16)
+            corr_ref[rows, width:] = (pr * gi - pi * gr).astype(BF16)
+        spec[...] = dot(corr_ref[pl.ds(base * shards, step * shards), :], table["conj"][...])
+        for i in range(0, step, 2):
             pairs = [
-                (spec[rows, 2 * j * width : (2 * j + 1) * width], spec[rows, (2 * j + 1) * width : (2 * j + 2) * width])
-                for j in range(2)
+                (spec[j * shards : (j + 1) * shards, :width], spec[j * shards : (j + 1) * shards, width:])
+                for j in (i, i + 1)
             ]
             part = signals_from(pairs, shards, width, cos, sin, last_ref) * scale
-            own_s[pl.ds(c, shards, stride=channels), :] = part[:, :width]
-            mir_s[pl.ds(channels - 1 - c, shards, stride=channels), :] = part[:, width:]
+            for j in range(2):
+                c = base + i + j
+                mir_s[pl.ds(channels - 1 - c, shards, stride=channels), :] = part[:, j * width : (j + 1) * width]
 
     for n1 in range(shards):
-        own_ref[:, n1 * width : (n1 + 1) * width] = own_s[n1 * channels : (n1 + 1) * channels, :]
         mir_ref[:, n1 * width : (n1 + 1) * width] = mir_s[n1 * channels : (n1 + 1) * channels, :].astype(BF16)
 
 
@@ -248,7 +261,7 @@
     table = table_views(table_ref, shards, width)
     last_ref = table["last_twice"]
     cos, sin = twist_ref[0], twist_ref[1]
-    step = 4
+    step = 8
     lane_channel = lax.broadcasted_iota(jnp.int32, (shards, width), 1) % channels
     first_s[...] = jnp.zeros_like(first_s)
 
@@ -292,11 +305,14 @@
     out_ref[:, both:, :] = extra_s[...].astype(BF16).reshape(shards, 8, width)
 
 
-def post_kernel(r_ref, g_ref, qs_ref, ks_ref, vs_ref, ends_ref, next_ref, taps_ref, mixed_ref, q_ref, k_ref, v_ref, ext, around):
+def post_kernel(r_ref, g_ref, qs_ref, ks_ref, vs_ref, ends_ref, next_ref, taps_ref, mixed_hbm, q_hbm, k_hbm, v_hbm, mixed_ref, q_ref, k_ref, v_ref, ext, around, sems):
     rows, channels = g_ref.shape
     group = (r_ref.shape[1] - 8) // 2
     count = 128 // group
     shape = (count, 8, 128)
+    size = channels // sems.shape[0]
+    pairs = ((mixed_ref, mixed_hbm), (q_ref, q_hbm), (k_ref, k_hbm), (v_ref, v_hbm))
+    copies = []
     mine = lax.broadcasted_iota(jnp.int32, shape, 2) // group == lax.broadcasted_iota(jnp.int32, shape, 0)
     for lane in range(0, channels, 128):
         lanes = pl.ds(lane, 128)
@@ -332,10 +348,41 @@
                 + taps_ref[p, 1:2, lanes] * ext[p, 1 : rows + 1, :]
                 + taps_ref[p, 2:3, lanes] * ext[p, 2 : rows + 2, :]
             ).astype(BF16)
-
-
-def add_kernel(near_ref, far_ref, out_ref):
-    out_ref[...] = near_ref[...] + far_ref[...].astype(F32)
+        if (lane + 128) % size == 0:
+            chunk = lane // size
+            lanes = pl.ds(chunk * size, size)
+            for p, (src, dst) in enumerate(pairs):
+                copies.append(pltpu.make_async_copy(src.at[:, lanes], dst.at[:, lanes], sems.at[chunk, p]))
+                copies[-1].start()
+    for copy in copies:
+        copy.wait()
+
+
+def lags_kernel(corr_ref, far_ref, table_ref, twist_ref, out_ref, own_s, spec):
+    channels, length = out_ref.shape
+    shards = twist_ref.shape[1]
+    width = length // shards
+    table = table_views(table_ref, shards, width)
+    scale = 1.0 / math.sqrt(length)
+    cos, sin = twist_ref[0], twist_ref[1]
+    step = 4
+
+    @pl.loop(0, channels, step=step)
+    def _(base):
+        spec[...] = dot(corr_ref[pl.ds(base * shards, step * shards), :], table["back"][...])
+        for i in range(0, step, 2):
+            pairs = [
+                (spec[j * shards : (j + 1) * shards, :width], spec[j * shards : (j + 1) * shards, width:])
+                for j in (i, i + 1)
+            ]
+            part = signals_from(pairs, shards, width, cos, sin, table["last_twice"]) * scale
+            for j in range(2):
+                c = base + i + j
+                own_s[pl.ds(c, shards, stride=channels), :] = part[:, j * width : (j + 1) * width]
+
+    for n1 in range(shards):
+        lanes = slice(n1 * width, (n1 + 1) * width)
+        out_ref[:, lanes] = own_s[n1 * channels : (n1 + 1) * channels, :] + far_ref[:, lanes].astype(F32)
 
 
 def per_device(query_proj, key_proj, value_proj, short_taps, skip_gain, long_filter, out_grad):
@@ -357,29 +404,33 @@
     previous, filter_sent = lax.optimization_barrier((previous, long_filter.astype(BF16)))
     filter_far = to_mirror(filter_sent)
     wide = shape((positions, width), BF16)
+    hbm, vmem = pl.BlockSpec(memory_space=pltpu.HBM), pl.BlockSpec(memory_space=pltpu.VMEM)
     query_short, key_short, value_short, send, own_ends = call(
         pre_kernel,
         (wide, wide, wide, shape((shards, 2 * channels, positions), BF16), shape((2, 2, width), BF16)),
         [
             *[pltpu.VMEM((positions, width), BF16)] * 4,
+            pltpu.VMEM(short_taps.shape, F32),
+            pltpu.VMEM((shards, 2 * channels, positions), BF16),
             pltpu.VMEM((3, positions + 8, 128), F32),
-            pltpu.SemaphoreType.DMA((4,)),
+            pltpu.SemaphoreType.DMA((4, 4)),
+            pltpu.SemaphoreType.DMA((5,)),
         ],
         flops=30 * positions * width,
         bytes_accessed=18 * positions * width,
-        in_specs=[pl.BlockSpec(memory_space=pltpu.HBM)] * 4
-        + [pl.BlockSpec(memory_space=pltpu.VMEM)] * 2,
-    )(*near, previous, short_taps)
+        in_specs=[hbm] * 5 + [vmem],
+        out_specs=(vmem, vmem, vmem, hbm, vmem),
+    )(*near, pltpu.with_memory_space_constraint(short_taps, pltpu.HBM), previous)
     received = lax.all_to_all(send, "seq", split_axis=0, concat_axis=0, tiled=True)
 
-    step = 4
+    step = 8
     spectrum = call(
         spectrum_kernel,
         shape((channels * shards, 2 * positions), F32),
         [
             pltpu.VMEM((shards * channels, positions), F32),
             pltpu.VMEM((shards * channels, positions), F32),
-            pltpu.VMEM((step * shards, 4 * positions), BF16),
+            pltpu.VMEM((4 * shards, 4 * positions), BF16),
         ],
         flops=SPEC_FLOPS,
         bytes_accessed=14 * channels * length,
@@ -389,25 +440,22 @@
     )(long_filter, filter_far, skip_gain, table, twist)
 
     received, spectrum = lax.optimization_barrier((received, spectrum))
-    spectra, lagged, lagged_back = call(
+    spectra, corr, lagged_back = call(
         corr_kernel,
         (
             shape((2 * channels * shards, 2 * positions), F32),
-            shape((channels, length), F32),
+            shape((channels * shards, 2 * positions), BF16),
             shape((channels, length), BF16),
         ),
         [
             pltpu.VMEM((shards * 2 * channels, positions), F32),
             pltpu.VMEM((shards * channels, positions), F32),
-            pltpu.VMEM((shards * channels, positions), F32),
             pltpu.VMEM((2 * step * shards, 2 * positions), BF16),
-            pltpu.VMEM((step * shards, 4 * positions), F32),
+            pltpu.VMEM((step * shards, 2 * positions), F32),
         ],
         flops=CORR_FLOPS,
         bytes_accessed=24 * channels * length,
     )(received, table, twist)
-    lagged_far = to_mirror(lagged_back)
-
     returned = call(
         mix_kernel,
         shape((shards, 2 * channels + 8, positions), BF16),
@@ -421,22 +469,34 @@
         flops=MIX_FLOPS,
         bytes_accessed=24 * channels * length,
     )(spectra, spectrum, table, twist)
+    lagged_back, returned = lax.optimization_barrier((lagged_back, returned))
+    lagged_far = to_mirror(lagged_back)
     result = lax.all_to_all(returned, "seq", split_axis=0, concat_axis=0, tiled=True)
 
     filter_grad = call(
-        add_kernel,
+        lags_kernel,
         shape((channels, length), F32),
+        [
+            pltpu.VMEM((shards * channels, positions), F32),
+            pltpu.VMEM((4 * shards, 2 * positions), F32),
+        ],
         flops=ADD_FLOPS,
         bytes_accessed=10 * channels * length,
-    )(lagged, lagged_far)
+    )(corr, lagged_far, table, twist)
     starts, filter_grad = lax.optimization_barrier((starts, filter_grad))
     following = passed_along(starts, "seq", -1)
     mixed_out, query_grad, key_grad, value_grad = call(
         post_kernel,
         (wide, wide, wide, wide),
-        [pltpu.VMEM((3, positions + 8, 128), F32), pltpu.VMEM((8, 128), F32)],
+        [
+            *[pltpu.VMEM((positions, width), BF16)] * 4,
+            pltpu.VMEM((3, positions + 8, 128), F32),
+            pltpu.VMEM((8, 128), F32),
+            pltpu.SemaphoreType.DMA((4, 4)),
+        ],
         flops=30 * positions * width,
         bytes_accessed=20 * positions * width,
+        out_specs=(hbm, hbm, hbm, hbm),
     )(result, out_grad, query_short, key_short, value_short, own_ends, following, short_taps)
     return (mixed_out, query_grad, key_grad, value_grad, filter_grad)
 

time: 88.1 us -> 84.7 us (0.961)
  waiting for transfers between devices: 33.5 us -> 30.6 us
    ppermute x2, waiting for transfers between devices: 11.4 us -> 17.7 us  [to_mirror(): lax.ppermute(array, ('seq', 'chan'), [(i, count - 1 - i) for i in range(c...]
    ppermute x2, waiting for transfers between devices: 7.4 us -> 3.53 us  [passed_along(): return lax.ppermute(array, axis, pairs)]
    all_to_all x1, waiting for transfers between devices: 5.04 us -> 1.28 us  [per_device(): lax.all_to_all(returned, 'seq', split_axis=0, concat_axis=0, tiled=True)]
    all_to_all x1, waiting for transfers between devices: 9.6 us -> 8.11 us  [per_device(): lax.all_to_all(send, 'seq', split_axis=0, concat_axis=0, tiled=True)]
    pallas_call x2, Pallas kernels: 2.61 us -> 4.02 us  [the longest x1 2.38 us: per_device(): call(lags_kernel, shape((channels, length), F32), [pltpu.VMEM((shards * c...]
    pallas_call x1, Pallas kernels: 3.54 us -> 2.36 us  [per_device(): call(corr_kernel, (shape((2 * channels * shards, 2 * positions), F32), sh...]
    unnamed x22 -> x20, local copies, waits for them, and re-layouts: 3.27 us -> 2.72 us
  transfers between devices with their start and end apart: 6 -> 6, of which waited for: 5 -> 5; matrix products, arithmetic and copies ran while one was open for 1% -> 1% of each run, Pallas kernels for 11% -> 10%
where the time goes in v2:
time: 84.7 us; the launch traced here: 84 us
  starting transfers between devices  33 us (39%)
  waiting for transfers between devices  30.6 us (36%)
  Pallas kernels  15.8 us (19%)
  local copies, waits for them, and re-layouts  2.72 us (3%)
  other arithmetic  1.07 us (1%)
    ppermute x2, waiting for transfers between devices, to_mirror(): lax.ppermute(array, ('seq', 'chan'), [(i, count - 1 - i) for i in range(c...  17.7 us
    ppermute x2, starting transfers between devices, to_mirror(): lax.ppermute(array, ('seq', 'chan'), [(i, count - 1 - i) for i in range(c...  14.5 us
    all_to_all x1, waiting for transfers between devices, per_device(): lax.all_to_all(send, 'seq', split_axis=0, concat_axis=0, tiled=True)  8.11 us
    all_to_all x1, starting transfers between devices, per_device(): lax.all_to_all(returned, 'seq', split_axis=0, concat_axis=0, tiled=True)  7.23 us
    ppermute x2, starting transfers between devices, passed_along(): return lax.ppermute(array, axis, pairs)  5.65 us
    all_to_all x1, starting transfers between devices, per_device(): lax.all_to_all(send, 'seq', split_axis=0, concat_axis=0, tiled=True)  5.62 us
    ppermute x2, waiting for transfers between devices, passed_along(): return lax.ppermute(array, axis, pairs)  3.53 us
    pallas_call x1, Pallas kernels, per_device(): call(pre_kernel, (wide, wide, wide, shape((shards, 2 * channels, position...  3.04 us
  transfers between devices with their start and end apart: 6, of which 5 were waited for; matrix products, arithmetic and copies ran while one was open for 1% of the time, Pallas kernels for 10%

profile of v2, /device:TPU:1, one launch (start us, length us, event | category | flops | bytes accessed | tf_op | source)
XLA Modules:
  0.0 84.0 jit_solution(16318422329799108829)
XLA Ops:
  0.6 0.0 copy-start.4
  0.6 0.0 copy-start.1
  0.7 0.0 copy-start.2
  0.7 0.0 copy-start.7
  0.7 1.0 %shard_map.128 = (bf16[3,2,1024]{2,1,0:T(2,128)(2,1)S(1)}, bf16[3,2,1024]{2,1,0:T(2,128)(2,1)S(1)}) custom-call(bf16[128,1024]{1,0:T(8,128)(2,1)} %q_hbm.3, bf16[128,1024]{1,0:T(8,128)(2,1)} %k_hbm.3, bf16[128,1024]{1,0:T(8,128)(2,1)} %v_hbm.3, bf16[128,1024]{1,0:T(8,128)(2,1)} %g_ref.1), custom_call_target="tpu_custom_call" | custom-call | bytes 204800 | tf_op jit(solution)/shard_map/pallas_call | solution.py:396
  1.7 4.4 %collective-permute-start = (bf16[3,2,1024]{2,1,0:T(2,128)(2,1)S(1)}, bf16[3,2,1024]{2,1,0:T(2,128)(2,1)S(1)}, u32[]{:S(2)}, u32[]{:S(2)}) collective-permute-start(bf16[3,2,1024]{2,1,0:T(2,128)(2,1)S(1)} %get-tuple-element.27), channel_id=1, source_target_pairs={{0,4},{4,8},{8,12},{12,16},{16,20},{20,24},{24,28},{28,32},{32,36}... | collective-permute-start | bytes 36872 | tf_op jit(solution)/shard_map/ppermute | solution.py:24
  6.1 1.1 %convert_element_type.3 = bf16[16,8192]{1,0:T(8,128)(2,1)S(1)} convert(f32[16,8192]{1,0:T(8,128)} %own_ref.1) | non-fusion elementwise | flops 131072 | bytes 786432 | tf_op jit(solution)/shard_map/convert_element_type | solution.py:404
  7.1 0.0 collective-permute-done.halo_ref
  7.1 11.7 %collective-permute-start.1 = (bf16[16,8192]{1,0:T(8,128)(2,1)S(1)}, bf16[16,8192]{1,0:T(8,128)(2,1)S(1)}, u32[]{:S(2)}, u32[]{:S(2)}) collective-permute-start(bf16[16,8192]{1,0:T(8,128)(2,1)S(1)} %convert_element_type.3), channel_id=1, source_target_pairs={{0,255},{1,254},{2,253},{3,252},{4,251},{5,250},{6,249},{7,248},{8... | collective-permute-start | bytes 786440 | tf_op jit(solution)/shard_map/ppermute | solution.py:29
  18.9 3.0 %shard_map.129 = (bf16[128,1024]{1,0:T(8,128)(2,1)S(1)}, bf16[128,1024]{1,0:T(8,128)(2,1)S(1)}, bf16[128,1024]{1,0:T(8,128)(2,1)S(1)}, bf16[64,32,128]{2,1,0:T(8,128)(2,1)}, bf16[2,2,1024]{2,1,0:T(2,128)(2,1)S(1)}) custom-call(bf16[128,1024]{1,0:T(8,128)(2,1)} %q_hbm.3, bf16[128,1024]{1,0:T(8,128)(2,1)} %k_hbm.3, bf16[128,1024]{1,0:T(8,128)(2,1)} %v_hbm.3, ...), custom_call_target="tpu_custom_call" | custom-call | flops 3932160 | bytes 2359296 | tf_op jit(solution)/shard_map/pallas_call | solution.py:408
  21.9 5.6 %all-to-all-start = ((bf16[64,32,128]{2,1,0:T(8,128)(2,1)}), bf16[64,32,128]{2,1,0:T(8,128)(2,1)S(1)}, u32[]{:S(2)}, u32[]{:S(2)}) async-start(bf16[64,32,128]{2,1,0:T(8,128)(2,1)} %get-tuple-element.29), calls=%async_computation | async-start | bytes 1048576 | tf_op jit(solution)/shard_map/all_to_all | solution.py:424
  27.5 6.1 %collective-permute-done.1.mir_ref = bf16[16,8192]{1,0:T(8,128)(2,1)S(1)} collective-permute-done((bf16[16,8192]{1,0:T(8,128)(2,1)S(1)}, bf16[16,8192]{1,0:T(8,128)(2,1)S(1)}, u32[]{:S(2)}, u32[]{:S(2)}) %collective-permute-start.1) | collective-permute-done | bytes 262176 | tf_op jit(solution)/shard_map/ppermute | solution.py:29
  33.7 0.0 copy-start.5
  33.7 0.7 copy-done.5
  34.4 0.0 copy-done.4
  34.4 0.0 copy-done.1
  34.4 0.0 copy-done.2
  34.4 0.0 copy-done.7
  34.4 0.0 copy-start.6
  34.4 0.9 %copy-done.6 = bf16[16,8192]{1,0:T(8,128)(2,1)S(1)} copy-done((bf16[16,8192]{1,0:T(8,128)(2,1)S(1)}, bf16[16,8192]{1,0:T(8,128)(2,1)}, u32[]{:S(2)}) %copy-start.6) | copy-done | bytes 262168
  35.3 2.6 %shard_map.130.spec_ref = f32[1024,256]{1,0:T(8,128)S(1)} custom-call(f32[16,8192]{1,0:T(8,128)S(1)} %copy-done.2, bf16[16,8192]{1,0:T(8,128)(2,1)S(1)} %copy-done.6, f32[1024]{0:T(1024)S(1)} %copy-done.7, bf16[1024,256]{1,0:T(8,128)(2,1)S(1)} %copy-done.1, f32[2,64,128]{2,1,0:T(8,128)S(1)} %copy-done.4), custom_call_target="tpu_custom_call" | custom-call | flops 17179869184 | bytes 1835008 | tf_op jit(solution)/shard_map/pallas_call | solution.py:427
  37.9 8.1 %all-to-all-done.x_ref = bf16[64,32,128]{2,1,0:T(8,128)(2,1)S(1)} async-done(((bf16[64,32,128]{2,1,0:T(8,128)(2,1)}), bf16[64,32,128]{2,1,0:T(8,128)(2,1)S(1)}, u32[]{:S(2)}, u32[]{:S(2)}) %all-to-all-start) | async-done | bytes 524320 | tf_op jit(solution)/shard_map/all_to_all | solution.py:424
  46.0 2.4 %shard_map.131 = (f32[2048,256]{1,0:T(8,128)S(1)}, bf16[1024,256]{1,0:T(8,128)(2,1)S(1)}, bf16[16,8192]{1,0:T(8,128)(2,1)S(1)}) custom-call(bf16[64,32,128]{2,1,0:T(8,128)(2,1)S(1)} %all-to-all-done.x_ref, bf16[1024,256]{1,0:T(8,128)(2,1)S(1)} %copy-done.1, f32[2,64,128]{2,1,0:T(8,128)S(1)} %copy-done.4), custom_call_target="tpu_custom_call" | custom-call | flops 536870912 | bytes 3145728 | tf_op jit(solution)/shard_map/pallas_call | solution.py:443
  48.4 0.0 copy-start.8
  48.4 2.8 %shard_map.132 = bf16[64,40,128]{2,1,0:T(8,128)(2,1)} custom-call(f32[2048,256]{1,0:T(8,128)S(1)} %get-tuple-element.33.spectra_ref, f32[1024,256]{1,0:T(8,128)S(1)} %shard_map.130.spec_ref, bf16[1024,256]{1,0:T(8,128)(2,1)S(1)} %copy-done.1, f32[2,64,128]{2,1,0:T(8,128)S(1)} %copy-done.4), custom_call_target="tpu_custom_call" | custom-call | flops 536870912 | bytes 3145728 | tf_op jit(solution)/shard_map/pallas_call | solution.py:459
  51.2 0.0 copy-done.8
  51.2 2.8 %collective-permute-start.2 = (bf16[16,8192]{1,0:T(8,128)(2,1)S(1)}, bf16[16,8192]{1,0:T(8,128)(2,1)S(1)}, u32[]{:S(2)}, u32[]{:S(2)}) collective-permute-start(bf16[16,8192]{1,0:T(8,128)(2,1)S(1)} %get-tuple-element.42), channel_id=1, source_target_pairs={{0,255},{1,254},{2,253},{3,252},{4,251},{5,250},{6,249},{7,248},{8... | collective-permute-start | bytes 786440 | tf_op jit(solution)/shard_map/ppermute | solution.py:29
  54.0 7.2 %all-to-all-start.1 = ((bf16[64,40,128]{2,1,0:T(8,128)(2,1)}), bf16[64,40,128]{2,1,0:T(8,128)(2,1)S(1)}, u32[]{:S(2)}, u32[]{:S(2)}) async-start(bf16[64,40,128]{2,1,0:T(8,128)(2,1)} %shard_map.132), calls=%async_computation.1 | async-start | bytes 1310720 | tf_op jit(solution)/shard_map/all_to_all | solution.py:474
  61.2 11.6 %collective-permute-done.2.far_ref = bf16[16,8192]{1,0:T(8,128)(2,1)S(1)} collective-permute-done((bf16[16,8192]{1,0:T(8,128)(2,1)S(1)}, bf16[16,8192]{1,0:T(8,128)(2,1)S(1)}, u32[]{:S(2)}, u32[]{:S(2)}) %collective-permute-start.2) | collective-permute-done | bytes 262176 | tf_op jit(solution)/shard_map/ppermute | solution.py:29
  72.8 0.0 copy-start.9
  72.8 1.0 %copy-done.9 = bf16[1024,256]{1,0:T(8,128)(2,1)S(1)} copy-done((bf16[1024,256]{1,0:T(8,128)(2,1)S(1)}, bf16[1024,256]{1,0:T(8,128)(2,1)}, u32[]{:S(2)}) %copy-start.9) | copy-done | bytes 524312
  73.9 0.0 copy-start
  73.9 0.0 copy-start.3
  73.9 2.4 %shard_map.133 = f32[16,8192]{1,0:T(8,128)} custom-call(bf16[1024,256]{1,0:T(8,128)(2,1)S(1)} %copy-done.9, bf16[16,8192]{1,0:T(8,128)(2,1)S(1)} %collective-permute-done.2.far_ref, bf16[1024,256]{1,0:T(8,128)(2,1)S(1)} %copy-done.1, f32[2,64,128]{2,1,0:T(8,128)S(1)} %copy-done.4), custom_call_target="tpu_custom_call" | custom-call | flops 17179869184 | bytes 1310720 | tf_op jit(solution)/shard_map/pallas_call | solution.py:476
  76.2 1.3 %collective-permute-start.3 = (bf16[3,2,1024]{2,1,0:T(2,128)(2,1)S(1)}, bf16[3,2,1024]{2,1,0:T(2,128)(2,1)S(1)}, u32[]{:S(2)}, u32[]{:S(2)}) collective-permute-start(bf16[3,2,1024]{2,1,0:T(2,128)(2,1)S(1)} %get-tuple-element.43), channel_id=1, source_target_pairs={{4,0},{8,4},{12,8},{16,12},{20,16},{24,20},{28,24},{32,28},{36,32}... | collective-permute-start | bytes 36872 | tf_op jit(solution)/shard_map/ppermute | solution.py:24
  77.5 3.5 %collective-permute-done.3.next_ref = bf16[3,2,1024]{2,1,0:T(2,128)(2,1)S(1)} collective-permute-done((bf16[3,2,1024]{2,1,0:T(2,128)(2,1)S(1)}, bf16[3,2,1024]{2,1,0:T(2,128)(2,1)S(1)}, u32[]{:S(2)}, u32[]{:S(2)}) %collective-permute-start.3) | collective-permute-done | bytes 12320 | tf_op jit(solution)/shard_map/ppermute | solution.py:24
  81.1 1.3 %all-to-all-done.1.r_ref = bf16[64,40,128]{2,1,0:T(8,128)(2,1)S(1)} async-done(((bf16[64,40,128]{2,1,0:T(8,128)(2,1)}), bf16[64,40,128]{2,1,0:T(8,128)(2,1)S(1)}, u32[]{:S(2)}, u32[]{:S(2)}) %all-to-all-start.1) | async-done | bytes 655392 | tf_op jit(solution)/shard_map/all_to_all | solution.py:474
  82.3 0.0 copy-done
  82.3 0.0 copy-done.3
  82.3 1.6 %shard_map.134 = (bf16[128,1024]{1,0:T(8,128)(2,1)}, bf16[128,1024]{1,0:T(8,128)(2,1)}, bf16[128,1024]{1,0:T(8,128)(2,1)}, bf16[128,1024]{1,0:T(8,128)(2,1)}) custom-call(bf16[64,40,128]{2,1,0:T(8,128)(2,1)S(1)} %all-to-all-done.1.r_ref, bf16[128,1024]{1,0:T(8,128)(2,1)S(1)} %copy-done, bf16[128,1024]{1,0:T(8,128)(2,1)S(1)} %get-tuple-element.36.qs_ref, ...), custom_call_target="tpu_custom_call" | custom-call | flops 3932160 | bytes 2621440 | tf_op jit(solution)/shard_map/pallas_call | solution.py:488
Async XLA Ops:
  0.6 33.7 %copy-start.4 = (f32[2,64,128]{2,1,0:T(8,128)S(1)}, f32[2,64,128]{2,1,0:T(8,128)}, u32[]{:S(2)}) copy-start(f32[2,64,128]{2,1,0:T(8,128)} %constant.5.clone.twist_ref) | copy-start | bytes 196612
  0.6 33.7 %copy-start.1 = (bf16[1024,256]{1,0:T(8,128)(2,1)S(1)}, bf16[1024,256]{1,0:T(8,128)(2,1)}, u32[]{:S(2)}) copy-start(bf16[1024,256]{1,0:T(8,128)(2,1)} %constant.4.clone.table_ref) | copy-start | bytes 1572868
  0.7 33.7 %copy-start.2 = (f32[16,8192]{1,0:T(8,128)S(1)}, f32[16,8192]{1,0:T(8,128)}, u32[]{:S(2)}) copy-start(f32[16,8192]{1,0:T(8,128)} %own_ref.1) | copy-start | bytes 1572868
  0.7 33.7 %copy-start.7 = (f32[1024]{0:T(1024)S(1)}, f32[1024]{0:T(1024)}, u32[]{:S(2)}) copy-start(f32[1024]{0:T(1024)} %skip_ref.1) | copy-start | bytes 12292
  1.7 5.5 %collective-permute-start = (bf16[3,2,1024]{2,1,0:T(2,128)(2,1)S(1)}, bf16[3,2,1024]{2,1,0:T(2,128)(2,1)S(1)}, u32[]{:S(2)}, u32[]{:S(2)}) collective-permute-start(bf16[3,2,1024]{2,1,0:T(2,128)(2,1)S(1)} %get-tuple-element.27), channel_id=1, source_target_pairs={{0,4},{4,8},{8,12},{12,16},{16,20},{20,24},{24,28},{28,32},{32,36}... | collective-permute-start | bytes 36872 | tf_op jit(solution)/shard_map/ppermute | solution.py:24
  7.1 26.5 %collective-permute-start.1 = (bf16[16,8192]{1,0:T(8,128)(2,1)S(1)}, bf16[16,8192]{1,0:T(8,128)(2,1)S(1)}, u32[]{:S(2)}, u32[]{:S(2)}) collective-permute-start(bf16[16,8192]{1,0:T(8,128)(2,1)S(1)} %convert_element_type.3), channel_id=1, source_target_pairs={{0,255},{1,254},{2,253},{3,252},{4,251},{5,250},{6,249},{7,248},{8... | collective-permute-start | bytes 786440 | tf_op jit(solution)/shard_map/ppermute | solution.py:29
  21.9 24.1 %all-to-all-start = ((bf16[64,32,128]{2,1,0:T(8,128)(2,1)}), bf16[64,32,128]{2,1,0:T(8,128)(2,1)S(1)}, u32[]{:S(2)}, u32[]{:S(2)}) async-start(bf16[64,32,128]{2,1,0:T(8,128)(2,1)} %get-tuple-element.29), calls=%async_computation | async-start | bytes 1048576 | tf_op jit(solution)/shard_map/all_to_all | solution.py:424
  33.7 0.7 copy-start.5
  34.4 1.0 %copy-start.6 = (bf16[16,8192]{1,0:T(8,128)(2,1)S(1)}, bf16[16,8192]{1,0:T(8,128)(2,1)}, u32[]{:S(2)}) copy-start(bf16[16,8192]{1,0:T(8,128)(2,1)} %copy-done.5) | copy-start | bytes 786436
  48.4 2.8 %copy-start.8 = (bf16[1024,256]{1,0:T(8,128)(2,1)}, bf16[1024,256]{1,0:T(8,128)(2,1)S(1)}, u32[]{:S(2)}) copy-start(bf16[1024,256]{1,0:T(8,128)(2,1)S(1)} %get-tuple-element.41.corr_ref) | copy-start | bytes 1572868
  51.2 21.6 %collective-permute-start.2 = (bf16[16,8192]{1,0:T(8,128)(2,1)S(1)}, bf16[16,8192]{1,0:T(8,128)(2,1)S(1)}, u32[]{:S(2)}, u32[]{:S(2)}) collective-permute-start(bf16[16,8192]{1,0:T(8,128)(2,1)S(1)} %get-tuple-element.42), channel_id=1, source_target_pairs={{0,255},{1,254},{2,253},{3,252},{4,251},{5,250},{6,249},{7,248},{8... | collective-permute-start | bytes 786440 | tf_op jit(solution)/shard_map/ppermute | solution.py:29
  54.0 28.3 %all-to-all-start.1 = ((bf16[64,40,128]{2,1,0:T(8,128)(2,1)}), bf16[64,40,128]{2,1,0:T(8,128)(2,1)S(1)}, u32[]{:S(2)}, u32[]{:S(2)}) async-start(bf16[64,40,128]{2,1,0:T(8,128)(2,1)} %shard_map.132), calls=%async_computation.1 | async-start | bytes 1310720 | tf_op jit(solution)/shard_map/all_to_all | solution.py:474
  72.8 1.0 %copy-start.9 = (bf16[1024,256]{1,0:T(8,128)(2,1)S(1)}, bf16[1024,256]{1,0:T(8,128)(2,1)}, u32[]{:S(2)}) copy-start(bf16[1024,256]{1,0:T(8,128)(2,1)} %copy-done.8) | copy-start | bytes 1572868
  73.9 8.5 %copy-start = (bf16[128,1024]{1,0:T(8,128)(2,1)S(1)}, bf16[128,1024]{1,0:T(8,128)(2,1)}, u32[]{:S(2)}) copy-start(bf16[128,1024]{1,0:T(8,128)(2,1)} %g_ref.1) | copy-start | bytes 786436
  73.9 8.5 %copy-start.3 = (f32[3,3,1024]{2,1,0:T(4,128)S(1)}, f32[3,3,1024]{2,1,0:T(4,128)}, u32[]{:S(2)}) copy-start(f32[3,3,1024]{2,1,0:T(4,128)} %taps_ref.1) | copy-start | bytes 110596
  76.2 4.8 %collective-permute-start.3 = (bf16[3,2,1024]{2,1,0:T(2,128)(2,1)S(1)}, bf16[3,2,1024]{2,1,0:T(2,128)(2,1)S(1)}, u32[]{:S(2)}, u32[]{:S(2)}) collective-permute-start(bf16[3,2,1024]{2,1,0:T(2,128)(2,1)S(1)} %get-tuple-element.43), channel_id=1, source_target_pairs={{4,0},{8,4},{12,8},{16,12},{20,16},{24,20},{28,24},{32,28},{36,32}... | collective-permute-start | bytes 36872 | tf_op jit(solution)/shard_map/ppermute | solution.py:24

commit v3 on v2

--- a/solution.py
+++ b/solution.py
@@ -15,6 +15,7 @@
 SPEC_FLOPS = 1 << 34
 CORR_FLOPS = 1 << 29
 MIX_FLOPS = 1 << 29
+STAGE_FLOPS = 1 << 20
 ADD_FLOPS = 1 << 34
 
 
@@ -102,29 +103,24 @@
             first_ref[p - 3] = held[p].astype(F32)[0:2].astype(BF16)
 
 
-def pre_kernel(
-    q_hbm, k_hbm, v_hbm, g_hbm, taps_hbm, halo_ref, qs_ref, ks_ref, vs_ref, send_hbm, ends_ref, q_ref, k_ref, v_ref, g_ref, taps_ref, send_ref, ext, sems, out_sems
-):
+def stage_kernel(q_hbm, k_hbm, v_hbm, g_hbm, taps_hbm, own_hbm, q_ref, k_ref, v_ref, g_ref, taps_ref, sent_ref, own_ref, sems):
+    pairs = ((own_hbm, own_ref), (q_hbm, q_ref), (k_hbm, k_ref), (v_hbm, v_ref), (g_hbm, g_ref), (taps_hbm, taps_ref))
+    copies = [pltpu.make_async_copy(src, dst, sems.at[p]) for p, (src, dst) in enumerate(pairs)]
+    for copy in copies:
+        copy.start()
+    copies[0].wait()
+    sent_ref[...] = own_ref[...].astype(BF16)
+    for copy in copies[1:]:
+        copy.wait()
+
+
+def pre_kernel(q_ref, k_ref, v_ref, g_ref, taps_ref, halo_ref, qs_ref, ks_ref, vs_ref, send_hbm, ends_ref, send_ref, ext, out_sems):
     rows, channels = q_ref.shape
     group = send_ref.shape[1] // 2
-    chunks = sems.shape[0]
+    chunks = out_sems.shape[0]
     size = channels // chunks
-    taps_copy = pltpu.make_async_copy(taps_hbm, taps_ref, out_sems.at[chunks])
-    taps_copy.start()
-    pairs = ((q_hbm, q_ref), (k_hbm, k_ref), (v_hbm, v_ref), (g_hbm, g_ref))
-    copies = []
-    for chunk in range(chunks):
-        lanes = pl.ds(chunk * size, size)
-        copies.append(
-            [pltpu.make_async_copy(src.at[:, lanes], dst.at[:, lanes], sems.at[chunk, p]) for p, (src, dst) in enumerate(pairs)]
-        )
-        for copy in copies[-1]:
-            copy.start()
-    taps_copy.wait()
     sends = []
     for chunk in range(chunks):
-        for copy in copies[chunk]:
-            copy.wait()
         for lane in range(chunk * size, (chunk + 1) * size, 128):
             lanes = pl.ds(lane, 128)
             shorts = []
@@ -213,7 +209,7 @@
     scale = 1.0 / math.sqrt(shards * width)
     xs[...] = x_ref[...].reshape(shards * both, width).astype(F32)
     cos, sin = twist_ref[0], twist_ref[1]
-    step = 8
+    step = 16
 
     @pl.loop(0, channels, step=step)
     def _(base):
@@ -261,7 +257,7 @@
     table = table_views(table_ref, shards, width)
     last_ref = table["last_twice"]
     cos, sin = twist_ref[0], twist_ref[1]
-    step = 8
+    step = 16
     lane_channel = lax.broadcasted_iota(jnp.int32, (shards, width), 1) % channels
     first_s[...] = jnp.zeros_like(first_s)
 
@@ -401,29 +397,34 @@
         in_specs=[pl.BlockSpec(memory_space=pltpu.HBM)] * 4,
     )(*near)
     previous = passed_along(ends, "seq", 1)
-    previous, filter_sent = lax.optimization_barrier((previous, long_filter.astype(BF16)))
-    filter_far = to_mirror(filter_sent)
     wide = shape((positions, width), BF16)
     hbm, vmem = pl.BlockSpec(memory_space=pltpu.HBM), pl.BlockSpec(memory_space=pltpu.VMEM)
+    far = [pltpu.with_memory_space_constraint(x, pltpu.HBM) for x in (out_grad, short_taps, long_filter)]
+    *staged, filter_sent = call(
+        stage_kernel,
+        (wide, wide, wide, wide, shape(short_taps.shape, F32), shape((channels, length), BF16)),
+        [pltpu.VMEM((channels, length), F32), pltpu.SemaphoreType.DMA((6,))],
+        flops=STAGE_FLOPS,
+        bytes_accessed=16 * positions * width,
+        in_specs=[hbm] * 6,
+    )(*near[:3], *far)
+    previous, filter_sent = lax.optimization_barrier((previous, filter_sent))
+    filter_far = to_mirror(filter_sent)
     query_short, key_short, value_short, send, own_ends = call(
         pre_kernel,
         (wide, wide, wide, shape((shards, 2 * channels, positions), BF16), shape((2, 2, width), BF16)),
         [
-            *[pltpu.VMEM((positions, width), BF16)] * 4,
-            pltpu.VMEM(short_taps.shape, F32),
             pltpu.VMEM((shards, 2 * channels, positions), BF16),
             pltpu.VMEM((3, positions + 8, 128), F32),
-            pltpu.SemaphoreType.DMA((4, 4)),
-            pltpu.SemaphoreType.DMA((5,)),
+            pltpu.SemaphoreType.DMA((4,)),
         ],
         flops=30 * positions * width,
         bytes_accessed=18 * positions * width,
-        in_specs=[hbm] * 5 + [vmem],
         out_specs=(vmem, vmem, vmem, hbm, vmem),
-    )(*near, pltpu.with_memory_space_constraint(short_taps, pltpu.HBM), previous)
+    )(*staged, previous)
     received = lax.all_to_all(send, "seq", split_axis=0, concat_axis=0, tiled=True)
 
-    step = 8
+    step = 16
     spectrum = call(
         spectrum_kernel,
         shape((channels * shards, 2 * positions), F32),
@@ -469,7 +470,6 @@
         flops=MIX_FLOPS,
         bytes_accessed=24 * channels * length,
     )(spectra, spectrum, table, twist)
-    lagged_back, returned = lax.optimization_barrier((lagged_back, returned))
     lagged_far = to_mirror(lagged_back)
     result = lax.all_to_all(returned, "seq", split_axis=0, concat_axis=0, tiled=True)
 

time: 84.7 us -> 83.4 us (0.985)
  other arithmetic: 1.07 us -> 0 us
  Pallas kernels: 15.8 us -> 14.9 us
    all_to_all x1, waiting for transfers between devices: 8.11 us -> 3.03 us  [per_device(): lax.all_to_all(send, 'seq', split_axis=0, concat_axis=0, tiled=True)]
    all_to_all x1, waiting for transfers between devices: 1.28 us -> 5.06 us  [per_device(): lax.all_to_all(returned, 'seq', split_axis=0, concat_axis=0, tiled=True)]
    ppermute x2, starting transfers between devices: 14.5 us -> 17.1 us  [to_mirror(): lax.ppermute(array, ('seq', 'chan'), [(i, count - 1 - i) for i in range(c...]
    all_to_all x1, starting transfers between devices: 7.23 us -> 5.27 us  [per_device(): lax.all_to_all(returned, 'seq', split_axis=0, concat_axis=0, tiled=True)]
    pallas_call x1, Pallas kernels: 3.04 us -> 1.46 us  [per_device(): call(pre_kernel, (wide, wide, wide, shape((shards, 2 * channels, position...]
    pallas_call x0 -> x1, Pallas kernels: none -> 1.4 us  [per_device(): call(stage_kernel, (wide, wide, wide, wide, shape(short_taps.shape, F32),...]
    ppermute x2, waiting for transfers between devices: 3.53 us -> 4.89 us  [passed_along(): return lax.ppermute(array, axis, pairs)]
    convert_element_type x1 -> x0, other arithmetic: 1.07 us -> none  [per_device(): long_filter.astype(BF16)]
  transfers between devices with their start and end apart: 6 -> 6, of which waited for: 5 -> 5; matrix products, arithmetic and copies ran while one was open for 1% -> 0% of each run, Pallas kernels for 10% -> 13%
where the time goes in v3:
time: 83.4 us; the launch traced here: 82.9 us
  starting transfers between devices  33.8 us (41%)
  waiting for transfers between devices  30 us (36%)
  Pallas kernels  14.9 us (18%)
  local copies, waits for them, and re-layouts  3.51 us (4%)
    ppermute x2, starting transfers between devices, to_mirror(): lax.ppermute(array, ('seq', 'chan'), [(i, count - 1 - i) for i in range(c...  17.1 us
    ppermute x2, waiting for transfers between devices, to_mirror(): lax.ppermute(array, ('seq', 'chan'), [(i, count - 1 - i) for i in range(c...  17 us
    ppermute x2, starting transfers between devices, passed_along(): return lax.ppermute(array, axis, pairs)  5.78 us
    all_to_all x1, starting transfers between devices, per_device(): lax.all_to_all(send, 'seq', split_axis=0, concat_axis=0, tiled=True)  5.62 us
    all_to_all x1, starting transfers between devices, per_device(): lax.all_to_all(returned, 'seq', split_axis=0, concat_axis=0, tiled=True)  5.27 us
    all_to_all x1, waiting for transfers between devices, per_device(): lax.all_to_all(returned, 'seq', split_axis=0, concat_axis=0, tiled=True)  5.06 us
    ppermute x2, waiting for transfers between devices, passed_along(): return lax.ppermute(array, axis, pairs)  4.89 us
    unnamed x20, local copies, waits for them, and re-layouts  3.51 us
  transfers between devices with their start and end apart: 6, of which 5 were waited for; matrix products, arithmetic and copies ran while one was open for 0% of the time, Pallas kernels for 13%

profile of v3, /device:TPU:1, one launch (start us, length us, event | category | flops | bytes accessed | tf_op | source)
XLA Modules:
  0.0 82.9 jit_solution(6268979611592997872)
XLA Ops:
  0.6 0.9 %shard_map.129 = (bf16[3,2,1024]{2,1,0:T(2,128)(2,1)S(1)}, bf16[3,2,1024]{2,1,0:T(2,128)(2,1)S(1)}) custom-call(bf16[128,1024]{1,0:T(8,128)(2,1)} %q_hbm.3, bf16[128,1024]{1,0:T(8,128)(2,1)} %k_hbm.3, bf16[128,1024]{1,0:T(8,128)(2,1)} %v_hbm.3, bf16[128,1024]{1,0:T(8,128)(2,1)} %g_ref.1), custom_call_target="tpu_custom_call" | custom-call | bytes 204800 | tf_op jit(solution)/shard_map/pallas_call | solution.py:392
  1.5 0.0 copy-start.1
  1.6 0.0 copy-start.2
  1.6 0.0 copy-start.4
  1.6 0.0 copy-start.7
  1.6 4.5 %collective-permute-start = (bf16[3,2,1024]{2,1,0:T(2,128)(2,1)S(1)}, bf16[3,2,1024]{2,1,0:T(2,128)(2,1)S(1)}, u32[]{:S(2)}, u32[]{:S(2)}) collective-permute-start(bf16[3,2,1024]{2,1,0:T(2,128)(2,1)S(1)} %get-tuple-element.36), channel_id=1, source_target_pairs={{0,4},{4,8},{8,12},{12,16},{16,20},{20,24},{24,28},{28,32},{32,36}... | collective-permute-start | bytes 36872 | tf_op jit(solution)/shard_map/ppermute | solution.py:25
  6.1 1.4 %shard_map.128 = (bf16[128,1024]{1,0:T(8,128)(2,1)S(1)}, bf16[128,1024]{1,0:T(8,128)(2,1)S(1)}, bf16[128,1024]{1,0:T(8,128)(2,1)S(1)}, bf16[128,1024]{1,0:T(8,12...) custom-call(bf16[128,1024]{1,0:T(8,128)(2,1)} %q_hbm.3, bf16[128,1024]{1,0:T(8,128)(2,1)} %k_hbm.3, ...), custom_call_target="tpu_custom_call" | custom-call | flops 1048576 | bytes 2097152 | tf_op jit(solution)/shard_map/pallas_call | solution.py:403
  7.5 0.0 collective-permute-done.halo_ref
  7.5 11.4 %collective-permute-start.1 = (bf16[16,8192]{1,0:T(8,128)(2,1)S(1)}, bf16[16,8192]{1,0:T(8,128)(2,1)S(1)}, u32[]{:S(2)}, u32[]{:S(2)}) collective-permute-start(bf16[16,8192]{1,0:T(8,128)(2,1)S(1)} %get-tuple-element.40), channel_id=1, source_target_pairs={{0,255},{1,254},{2,253},{3,252},{4,251},{5,250},{6,249},{7,248},{8... | collective-permute-start | bytes 786440 | tf_op jit(solution)/shard_map/ppermute | solution.py:30
  18.9 1.5 %shard_map.130 = (bf16[128,1024]{1,0:T(8,128)(2,1)S(1)}, bf16[128,1024]{1,0:T(8,128)(2,1)S(1)}, bf16[128,1024]{1,0:T(8,128)(2,1)S(1)}, bf16[64,32,128]{2,1,0:T(8,128)(2,1)}, bf16[2,2,1024]{2,1,0:T(2,128)(2,1)S(1)}) custom-call(bf16[128,1024]{1,0:T(8,128)(2,1)S(1)} %get-tuple-element.31.q_ref, bf16[128,1024]{1,0:T(8,128)(2,1)S(1)} %get-tuple-element.32.k_ref, ...), custom_call_target="tpu_custom_call" | custom-call | flops 3932160 | bytes 2359296 | tf_op jit(solution)/shard_map/pallas_call | solution.py:413
  20.4 5.6 %all-to-all-start = ((bf16[64,32,128]{2,1,0:T(8,128)(2,1)}), bf16[64,32,128]{2,1,0:T(8,128)(2,1)S(1)}, u32[]{:S(2)}, u32[]{:S(2)}) async-start(bf16[64,32,128]{2,1,0:T(8,128)(2,1)} %get-tuple-element.39), calls=%async_computation | async-start | bytes 1048576 | tf_op jit(solution)/shard_map/all_to_all | solution.py:425
  26.0 10.3 %collective-permute-done.1.mir_ref = bf16[16,8192]{1,0:T(8,128)(2,1)S(1)} collective-permute-done((bf16[16,8192]{1,0:T(8,128)(2,1)S(1)}, bf16[16,8192]{1,0:T(8,128)(2,1)S(1)}, u32[]{:S(2)}, u32[]{:S(2)}) %collective-permute-start.1) | collective-permute-done | bytes 262176 | tf_op jit(solution)/shard_map/ppermute | solution.py:30
  36.3 0.0 copy-start.5
  36.3 0.7 copy-done.5
  37.0 0.0 copy-done.1
  37.0 0.0 copy-done.2
  37.0 0.0 copy-done.4
  37.0 0.0 copy-done.7
  37.0 0.0 copy-start.6
  37.0 0.9 %copy-done.6 = bf16[16,8192]{1,0:T(8,128)(2,1)S(1)} copy-done((bf16[16,8192]{1,0:T(8,128)(2,1)S(1)}, bf16[16,8192]{1,0:T(8,128)(2,1)}, u32[]{:S(2)}) %copy-start.6) | copy-done | bytes 262168
  37.9 2.6 %shard_map.131.spec_ref = f32[1024,256]{1,0:T(8,128)S(1)} custom-call(f32[16,8192]{1,0:T(8,128)S(1)} %copy-done.1, bf16[16,8192]{1,0:T(8,128)(2,1)S(1)} %copy-done.6, f32[1024]{0:T(1024)S(1)} %copy-done.7, bf16[1024,256]{1,0:T(8,128)(2,1)S(1)} %copy-done.2, f32[2,64,128]{2,1,0:T(8,128)S(1)} %copy-done.4), custom_call_target="tpu_custom_call" | custom-call | flops 17179869184 | bytes 1835008 | tf_op jit(solution)/shard_map/pallas_call | solution.py:428
  40.5 3.0 %all-to-all-done.x_ref = bf16[64,32,128]{2,1,0:T(8,128)(2,1)S(1)} async-done(((bf16[64,32,128]{2,1,0:T(8,128)(2,1)}), bf16[64,32,128]{2,1,0:T(8,128)(2,1)S(1)}, u32[]{:S(2)}, u32[]{:S(2)}) %all-to-all-start) | async-done | bytes 524320 | tf_op jit(solution)/shard_map/all_to_all | solution.py:425
  43.6 1.9 %shard_map.132 = (f32[2048,256]{1,0:T(8,128)S(1)}, bf16[1024,256]{1,0:T(8,128)(2,1)S(1)}, bf16[16,8192]{1,0:T(8,128)(2,1)S(1)}) custom-call(bf16[64,32,128]{2,1,0:T(8,128)(2,1)S(1)} %all-to-all-done.x_ref, bf16[1024,256]{1,0:T(8,128)(2,1)S(1)} %copy-done.2, f32[2,64,128]{2,1,0:T(8,128)S(1)} %copy-done.4), custom_call_target="tpu_custom_call" | custom-call | flops 536870912 | bytes 3145728 | tf_op jit(solution)/shard_map/pallas_call | solution.py:444
  45.5 0.0 copy-start.8
  45.5 0.8 copy-done.8
  46.3 5.7 %collective-permute-start.2 = (bf16[16,8192]{1,0:T(8,128)(2,1)S(1)}, bf16[16,8192]{1,0:T(8,128)(2,1)S(1)}, u32[]{:S(2)}, u32[]{:S(2)}) collective-permute-start(bf16[16,8192]{1,0:T(8,128)(2,1)S(1)} %get-tuple-element.50), channel_id=1, source_target_pairs={{0,255},{1,254},{2,253},{3,252},{4,251},{5,250},{6,249},{7,248},{8... | collective-permute-start | bytes 786440 | tf_op jit(solution)/shard_map/ppermute | solution.py:30
  52.0 2.6 %shard_map.133 = bf16[64,40,128]{2,1,0:T(8,128)(2,1)} custom-call(f32[2048,256]{1,0:T(8,128)S(1)} %get-tuple-element.42.spectra_ref, f32[1024,256]{1,0:T(8,128)S(1)} %shard_map.131.spec_ref, bf16[1024,256]{1,0:T(8,128)(2,1)S(1)} %copy-done.2, f32[2,64,128]{2,1,0:T(8,128)S(1)} %copy-done.4), custom_call_target="tpu_custom_call" | custom-call | flops 536870912 | bytes 3145728 | tf_op jit(solution)/shard_map/pallas_call | solution.py:460
  54.6 5.3 %all-to-all-start.1 = ((bf16[64,40,128]{2,1,0:T(8,128)(2,1)}), bf16[64,40,128]{2,1,0:T(8,128)(2,1)S(1)}, u32[]{:S(2)}, u32[]{:S(2)}) async-start(bf16[64,40,128]{2,1,0:T(8,128)(2,1)} %shard_map.133), calls=%async_computation.1 | async-start | bytes 1310720 | tf_op jit(solution)/shard_map/all_to_all | solution.py:474
  59.9 6.7 %collective-permute-done.2.far_ref = bf16[16,8192]{1,0:T(8,128)(2,1)S(1)} collective-permute-done((bf16[16,8192]{1,0:T(8,128)(2,1)S(1)}, bf16[16,8192]{1,0:T(8,128)(2,1)S(1)}, u32[]{:S(2)}, u32[]{:S(2)}) %collective-permute-start.2) | collective-permute-done | bytes 262176 | tf_op jit(solution)/shard_map/ppermute | solution.py:30
  66.6 0.0 copy-start.9
  66.6 1.0 %copy-done.9 = bf16[1024,256]{1,0:T(8,128)(2,1)S(1)} copy-done((bf16[1024,256]{1,0:T(8,128)(2,1)S(1)}, bf16[1024,256]{1,0:T(8,128)(2,1)}, u32[]{:S(2)}) %copy-start.9) | copy-done | bytes 524312
  67.6 0.0 copy-start
  67.6 0.0 copy-start.3
  67.6 2.4 %shard_map.134 = f32[16,8192]{1,0:T(8,128)} custom-call(bf16[1024,256]{1,0:T(8,128)(2,1)S(1)} %copy-done.9, bf16[16,8192]{1,0:T(8,128)(2,1)S(1)} %collective-permute-done.2.far_ref, bf16[1024,256]{1,0:T(8,128)(2,1)S(1)} %copy-done.2, f32[2,64,128]{2,1,0:T(8,128)S(1)} %copy-done.4), custom_call_target="tpu_custom_call" | custom-call | flops 17179869184 | bytes 1310720 | tf_op jit(solution)/shard_map/pallas_call | solution.py:476
  70.0 1.3 %collective-permute-start.3 = (bf16[3,2,1024]{2,1,0:T(2,128)(2,1)S(1)}, bf16[3,2,1024]{2,1,0:T(2,128)(2,1)S(1)}, u32[]{:S(2)}, u32[]{:S(2)}) collective-permute-start(bf16[3,2,1024]{2,1,0:T(2,128)(2,1)S(1)} %get-tuple-element.51), channel_id=1, source_target_pairs={{4,0},{8,4},{12,8},{16,12},{20,16},{24,20},{28,24},{32,28},{36,32}... | collective-permute-start | bytes 36872 | tf_op jit(solution)/shard_map/ppermute | solution.py:25
  71.3 4.9 %collective-permute-done.3.next_ref = bf16[3,2,1024]{2,1,0:T(2,128)(2,1)S(1)} collective-permute-done((bf16[3,2,1024]{2,1,0:T(2,128)(2,1)S(1)}, bf16[3,2,1024]{2,1,0:T(2,128)(2,1)S(1)}, u32[]{:S(2)}, u32[]{:S(2)}) %collective-permute-start.3) | collective-permute-done | bytes 12320 | tf_op jit(solution)/shard_map/ppermute | solution.py:25
  76.2 5.1 %all-to-all-done.1.r_ref = bf16[64,40,128]{2,1,0:T(8,128)(2,1)S(1)} async-done(((bf16[64,40,128]{2,1,0:T(8,128)(2,1)}), bf16[64,40,128]{2,1,0:T(8,128)(2,1)S(1)}, u32[]{:S(2)}, u32[]{:S(2)}) %all-to-all-start.1) | async-done | bytes 655392 | tf_op jit(solution)/shard_map/all_to_all | solution.py:474
  81.2 0.0 copy-done
  81.3 0.0 copy-done.3
  81.3 1.6 %shard_map.135 = (bf16[128,1024]{1,0:T(8,128)(2,1)}, bf16[128,1024]{1,0:T(8,128)(2,1)}, bf16[128,1024]{1,0:T(8,128)(2,1)}, bf16[128,1024]{1,0:T(8,128)(2,1)}) custom-call(bf16[64,40,128]{2,1,0:T(8,128)(2,1)S(1)} %all-to-all-done.1.r_ref, bf16[128,1024]{1,0:T(8,128)(2,1)S(1)} %copy-done, bf16[128,1024]{1,0:T(8,128)(2,1)S(1)} %get-tuple-element.44.qs_ref, ...), custom_call_target="tpu_custom_call" | custom-call | flops 3932160 | bytes 2621440 | tf_op jit(solution)/shard_map/pallas_call | solution.py:488
Async XLA Ops:
  1.5 35.4 %copy-start.1 = (f32[16,8192]{1,0:T(8,128)S(1)}, f32[16,8192]{1,0:T(8,128)}, u32[]{:S(2)}) copy-start(f32[16,8192]{1,0:T(8,128)} %own_ref.1) | copy-start | bytes 1572868
  1.6 35.4 %copy-start.2 = (bf16[1024,256]{1,0:T(8,128)(2,1)S(1)}, bf16[1024,256]{1,0:T(8,128)(2,1)}, u32[]{:S(2)}) copy-start(bf16[1024,256]{1,0:T(8,128)(2,1)} %constant.4.clone.table_ref) | copy-start | bytes 1572868
  1.6 35.4 %copy-start.4 = (f32[2,64,128]{2,1,0:T(8,128)S(1)}, f32[2,64,128]{2,1,0:T(8,128)}, u32[]{:S(2)}) copy-start(f32[2,64,128]{2,1,0:T(8,128)} %constant.5.clone.twist_ref) | copy-start | bytes 196612
  1.6 35.4 %copy-start.7 = (f32[1024]{0:T(1024)S(1)}, f32[1024]{0:T(1024)}, u32[]{:S(2)}) copy-start(f32[1024]{0:T(1024)} %skip_ref.1) | copy-start | bytes 12292
  1.6 5.9 %collective-permute-start = (bf16[3,2,1024]{2,1,0:T(2,128)(2,1)S(1)}, bf16[3,2,1024]{2,1,0:T(2,128)(2,1)S(1)}, u32[]{:S(2)}, u32[]{:S(2)}) collective-permute-start(bf16[3,2,1024]{2,1,0:T(2,128)(2,1)S(1)} %get-tuple-element.36), channel_id=1, source_target_pairs={{0,4},{4,8},{8,12},{12,16},{16,20},{20,24},{24,28},{28,32},{32,36}... | collective-permute-start | bytes 36872 | tf_op jit(solution)/shard_map/ppermute | solution.py:25
  7.5 28.8 %collective-permute-start.1 = (bf16[16,8192]{1,0:T(8,128)(2,1)S(1)}, bf16[16,8192]{1,0:T(8,128)(2,1)S(1)}, u32[]{:S(2)}, u32[]{:S(2)}) collective-permute-start(bf16[16,8192]{1,0:T(8,128)(2,1)S(1)} %get-tuple-element.40), channel_id=1, source_target_pairs={{0,255},{1,254},{2,253},{3,252},{4,251},{5,250},{6,249},{7,248},{8... | collective-permute-start | bytes 786440 | tf_op jit(solution)/shard_map/ppermute | solution.py:30
  20.4 23.2 %all-to-all-start = ((bf16[64,32,128]{2,1,0:T(8,128)(2,1)}), bf16[64,32,128]{2,1,0:T(8,128)(2,1)S(1)}, u32[]{:S(2)}, u32[]{:S(2)}) async-start(bf16[64,32,128]{2,1,0:T(8,128)(2,1)} %get-tuple-element.39), calls=%async_computation | async-start | bytes 1048576 | tf_op jit(solution)/shard_map/all_to_all | solution.py:425
  36.3 0.7 copy-start.5
  37.0 1.0 %copy-start.6 = (bf16[16,8192]{1,0:T(8,128)(2,1)S(1)}, bf16[16,8192]{1,0:T(8,128)(2,1)}, u32[]{:S(2)}) copy-start(bf16[16,8192]{1,0:T(8,128)(2,1)} %copy-done.5) | copy-start | bytes 786436
  45.5 0.8 copy-start.8
  46.3 20.3 %collective-permute-start.2 = (bf16[16,8192]{1,0:T(8,128)(2,1)S(1)}, bf16[16,8192]{1,0:T(8,128)(2,1)S(1)}, u32[]{:S(2)}, u32[]{:S(2)}) collective-permute-start(bf16[16,8192]{1,0:T(8,128)(2,1)S(1)} %get-tuple-element.50), channel_id=1, source_target_pairs={{0,255},{1,254},{2,253},{3,252},{4,251},{5,250},{6,249},{7,248},{8... | collective-permute-start | bytes 786440 | tf_op jit(solution)/shard_map/ppermute | solution.py:30
  54.6 26.7 %all-to-all-start.1 = ((bf16[64,40,128]{2,1,0:T(8,128)(2,1)}), bf16[64,40,128]{2,1,0:T(8,128)(2,1)S(1)}, u32[]{:S(2)}, u32[]{:S(2)}) async-start(bf16[64,40,128]{2,1,0:T(8,128)(2,1)} %shard_map.133), calls=%async_computation.1 | async-start | bytes 1310720 | tf_op jit(solution)/shard_map/all_to_all | solution.py:474
  66.6 1.0 %copy-start.9 = (bf16[1024,256]{1,0:T(8,128)(2,1)S(1)}, bf16[1024,256]{1,0:T(8,128)(2,1)}, u32[]{:S(2)}) copy-start(bf16[1024,256]{1,0:T(8,128)(2,1)} %copy-done.8) | copy-start | bytes 1572868
  67.6 13.6 %copy-start = (bf16[128,1024]{1,0:T(8,128)(2,1)S(1)}, bf16[128,1024]{1,0:T(8,128)(2,1)}, u32[]{:S(2)}) copy-start(bf16[128,1024]{1,0:T(8,128)(2,1)} %g_ref.1) | copy-start | bytes 786436
  67.6 13.6 %copy-start.3 = (f32[3,3,1024]{2,1,0:T(4,128)S(1)}, f32[3,3,1024]{2,1,0:T(4,128)}, u32[]{:S(2)}) copy-start(f32[3,3,1024]{2,1,0:T(4,128)} %taps_ref.1) | copy-start | bytes 110596
  70.0 6.2 %collective-permute-start.3 = (bf16[3,2,1024]{2,1,0:T(2,128)(2,1)S(1)}, bf16[3,2,1024]{2,1,0:T(2,128)(2,1)S(1)}, u32[]{:S(2)}, u32[]{:S(2)}) collective-permute-start(bf16[3,2,1024]{2,1,0:T(2,128)(2,1)S(1)} %get-tuple-element.51), channel_id=1, source_target_pairs={{4,0},{8,4},{12,8},{16,12},{20,16},{24,20},{28,24},{32,28},{36,32}... | collective-permute-start | bytes 36872 | tf_op jit(solution)/shard_map/ppermute | solution.py:25

commit v4 on v3

--- a/solution.py
+++ b/solution.py
@@ -201,7 +201,7 @@
     return parts[:shards] + parts[shards:]
 
 
-def corr_kernel(x_ref, table_ref, twist_ref, spectra_ref, corr_ref, mir_ref, xs, mir_s, lhs, spec):
+def corr_kernel(x_ref, table_ref, twist_ref, spectra_ref, mir_ref, corr_ref, xs, mir_s, lhs, spec):
     shards, both, width = x_ref.shape
     channels = both // 2
     table = table_views(table_ref, shards, width)
@@ -354,24 +354,46 @@
         copy.wait()
 
 
-def lags_kernel(corr_ref, far_ref, table_ref, twist_ref, out_ref, own_s, spec):
-    channels, length = out_ref.shape
-    shards = twist_ref.shape[1]
-    width = length // shards
+def lags_kernel(x_ref, far_ref, table_ref, twist_ref, out_ref, corr_ref, xs, own_s, lhs, spec):
+    shards, both, width = x_ref.shape
+    channels = both // 2
     table = table_views(table_ref, shards, width)
-    scale = 1.0 / math.sqrt(length)
+    first_ref, last_ref = table["first_twice"], table["last_twice"]
+    scale = 1.0 / math.sqrt(shards * width)
+    xs[...] = x_ref[...].reshape(shards * both, width).astype(F32)
     cos, sin = twist_ref[0], twist_ref[1]
-    step = 4
+    step = 16
 
     @pl.loop(0, channels, step=step)
     def _(base):
+        for i in range(step):
+            c = base + i
+            product = xs[pl.ds(c, shards, stride=both), :].astype(BF16)
+            gate = xs[pl.ds(channels + c, shards, stride=both), :].astype(BF16)
+            rhs = jnp.concatenate([product, gate], 1)
+            part = dot(first_ref[...], jnp.concatenate([rhs, rhs], 0))
+            for j in range(2):
+                real = part[:shards, j * width : (j + 1) * width]
+                imag = part[shards:, j * width : (j + 1) * width]
+                rows = pl.ds((2 * i + j) * shards, shards)
+                lhs[rows, :width] = (real * cos + imag * sin).astype(BF16)
+                lhs[rows, width:] = (imag * cos - real * sin).astype(BF16)
+        both_spec = dot(lhs[...], table["forth"][...])
+        for i in range(step):
+            pr = both_spec[2 * i * shards : (2 * i + 1) * shards, :width]
+            pi = both_spec[2 * i * shards : (2 * i + 1) * shards, width:]
+            gr = both_spec[(2 * i + 1) * shards : (2 * i + 2) * shards, :width]
+            gi = both_spec[(2 * i + 1) * shards : (2 * i + 2) * shards, width:]
+            rows = pl.ds((base + i) * shards, shards)
+            corr_ref[rows, :width] = (pr * gr + pi * gi).astype(BF16)
+            corr_ref[rows, width:] = (pr * gi - pi * gr).astype(BF16)
         spec[...] = dot(corr_ref[pl.ds(base * shards, step * shards), :], table["back"][...])
         for i in range(0, step, 2):
             pairs = [
                 (spec[j * shards : (j + 1) * shards, :width], spec[j * shards : (j + 1) * shards, width:])
                 for j in (i, i + 1)
             ]
-            part = signals_from(pairs, shards, width, cos, sin, table["last_twice"]) * scale
+            part = signals_from(pairs, shards, width, cos, sin, last_ref) * scale
             for j in range(2):
                 c = base + i + j
                 own_s[pl.ds(c, shards, stride=channels), :] = part[:, j * width : (j + 1) * width]
@@ -441,14 +463,14 @@
     )(long_filter, filter_far, skip_gain, table, twist)
 
     received, spectrum = lax.optimization_barrier((received, spectrum))
-    spectra, corr, lagged_back = call(
+    spectra, lagged_back = call(
         corr_kernel,
         (
             shape((2 * channels * shards, 2 * positions), F32),
-            shape((channels * shards, 2 * positions), BF16),
             shape((channels, length), BF16),
         ),
         [
+            pltpu.VMEM((channels * shards, 2 * positions), BF16),
             pltpu.VMEM((shards * 2 * channels, positions), F32),
             pltpu.VMEM((shards * channels, positions), F32),
             pltpu.VMEM((2 * step * shards, 2 * positions), BF16),
@@ -473,18 +495,22 @@
     lagged_far = to_mirror(lagged_back)
     result = lax.all_to_all(returned, "seq", split_axis=0, concat_axis=0, tiled=True)
 
+    starts, lagged_far = lax.optimization_barrier((starts, lagged_far))
+    following = passed_along(starts, "seq", -1)
     filter_grad = call(
         lags_kernel,
         shape((channels, length), F32),
         [
+            pltpu.VMEM((channels * shards, 2 * positions), BF16),
+            pltpu.VMEM((shards * 2 * channels, positions), F32),
             pltpu.VMEM((shards * channels, positions), F32),
-            pltpu.VMEM((4 * shards, 2 * positions), F32),
+            pltpu.VMEM((2 * step * shards, 2 * positions), BF16),
+            pltpu.VMEM((step * shards, 2 * positions), F32),
         ],
         flops=ADD_FLOPS,
         bytes_accessed=10 * channels * length,
-    )(corr, lagged_far, table, twist)
-    starts, filter_grad = lax.optimization_barrier((starts, filter_grad))
-    following = passed_along(starts, "seq", -1)
+    )(received, lagged_far, table, twist)
+    following, filter_grad = lax.optimization_barrier((following, filter_grad))
     mixed_out, query_grad, key_grad, value_grad = call(
         post_kernel,
         (wide, wide, wide, wide),

time: 83.4 us -> 82.6 us (level)
  local copies, waits for them, and re-layouts: 3.51 us -> 1.68 us
    unnamed x20 -> x16, local copies, waits for them, and re-layouts: 3.51 us -> 1.68 us
where the time goes in v4:
time: 82.6 us; the launch traced here: 82.1 us
  starting transfers between devices  34 us (41%)
  waiting for transfers between devices  30.6 us (37%)
  Pallas kernels  15.1 us (18%)
  local copies, waits for them, and re-layouts  1.68 us (2%)
    ppermute x2, starting transfers between devices, to_mirror(): lax.ppermute(array, ('seq', 'chan'), [(i, count - 1 - i) for i in range(c...  17.2 us
    ppermute x2, waiting for transfers between devices, to_mirror(): lax.ppermute(array, ('seq', 'chan'), [(i, count - 1 - i) for i in range(c...  17.1 us
    ppermute x2, starting transfers between devices, passed_along(): return lax.ppermute(array, axis, pairs)  5.92 us
    all_to_all x1, starting transfers between devices, per_device(): lax.all_to_all(send, 'seq', split_axis=0, concat_axis=0, tiled=True)  5.62 us
    ppermute x2, waiting for transfers between devices, passed_along(): return lax.ppermute(array, axis, pairs)  5.44 us
    all_to_all x1, starting transfers between devices, per_device(): lax.all_to_all(returned, 'seq', split_axis=0, concat_axis=0, tiled=True)  5.27 us
    all_to_all x1, waiting for transfers between devices, per_device(): lax.all_to_all(returned, 'seq', split_axis=0, concat_axis=0, tiled=True)  5.04 us
    all_to_all x1, waiting for transfers between devices, per_device(): lax.all_to_all(send, 'seq', split_axis=0, concat_axis=0, tiled=True)  3.03 us
  transfers between devices with their start and end apart: 6, of which 5 were waited for; matrix products, arithmetic and copies ran while one was open for 0% of the time, Pallas kernels for 13%

profile of v4, /device:TPU:1, one launch (start us, length us, event | category | flops | bytes accessed | tf_op | source)
XLA Modules:
  0.0 82.1 jit_solution(12328478749980791908)
XLA Ops:
  0.6 0.9 %shard_map.129 = (bf16[3,2,1024]{2,1,0:T(2,128)(2,1)S(1)}, bf16[3,2,1024]{2,1,0:T(2,128)(2,1)S(1)}) custom-call(bf16[128,1024]{1,0:T(8,128)(2,1)} %q_hbm.3, bf16[128,1024]{1,0:T(8,128)(2,1)} %k_hbm.3, bf16[128,1024]{1,0:T(8,128)(2,1)} %v_hbm.3, bf16[128,1024]{1,0:T(8,128)(2,1)} %g_ref.1), custom_call_target="tpu_custom_call" | custom-call | bytes 204800 | tf_op jit(solution)/shard_map/pallas_call | solution.py:414
  1.5 0.0 copy-start.1
  1.6 0.0 copy-start.2
  1.6 0.0 copy-start.4
  1.6 0.0 copy-start.7
  1.6 4.5 %collective-permute-start = (bf16[3,2,1024]{2,1,0:T(2,128)(2,1)S(1)}, bf16[3,2,1024]{2,1,0:T(2,128)(2,1)S(1)}, u32[]{:S(2)}, u32[]{:S(2)}) collective-permute-start(bf16[3,2,1024]{2,1,0:T(2,128)(2,1)S(1)} %get-tuple-element.37), channel_id=1, source_target_pairs={{0,4},{4,8},{8,12},{12,16},{16,20},{20,24},{24,28},{28,32},{32,36}... | collective-permute-start | bytes 36872 | tf_op jit(solution)/shard_map/ppermute | solution.py:25
  6.1 1.4 %shard_map.128 = (bf16[128,1024]{1,0:T(8,128)(2,1)S(1)}, bf16[128,1024]{1,0:T(8,128)(2,1)S(1)}, bf16[128,1024]{1,0:T(8,128)(2,1)S(1)}, bf16[128,1024]{1,0:T(8,12...) custom-call(bf16[128,1024]{1,0:T(8,128)(2,1)} %q_hbm.3, bf16[128,1024]{1,0:T(8,128)(2,1)} %k_hbm.3, ...), custom_call_target="tpu_custom_call" | custom-call | flops 1048576 | bytes 2097152 | tf_op jit(solution)/shard_map/pallas_call | solution.py:425
  7.5 0.0 collective-permute-done.halo_ref
  7.5 11.4 %collective-permute-start.1 = (bf16[16,8192]{1,0:T(8,128)(2,1)S(1)}, bf16[16,8192]{1,0:T(8,128)(2,1)S(1)}, u32[]{:S(2)}, u32[]{:S(2)}) collective-permute-start(bf16[16,8192]{1,0:T(8,128)(2,1)S(1)} %get-tuple-element.41), channel_id=1, source_target_pairs={{0,255},{1,254},{2,253},{3,252},{4,251},{5,250},{6,249},{7,248},{8... | collective-permute-start | bytes 786440 | tf_op jit(solution)/shard_map/ppermute | solution.py:30
  18.9 1.5 %shard_map.130 = (bf16[128,1024]{1,0:T(8,128)(2,1)S(1)}, bf16[128,1024]{1,0:T(8,128)(2,1)S(1)}, bf16[128,1024]{1,0:T(8,128)(2,1)S(1)}, bf16[64,32,128]{2,1,0:T(8,128)(2,1)}, bf16[2,2,1024]{2,1,0:T(2,128)(2,1)S(1)}) custom-call(bf16[128,1024]{1,0:T(8,128)(2,1)S(1)} %get-tuple-element.32.q_ref, bf16[128,1024]{1,0:T(8,128)(2,1)S(1)} %get-tuple-element.33.k_ref, ...), custom_call_target="tpu_custom_call" | custom-call | flops 3932160 | bytes 2359296 | tf_op jit(solution)/shard_map/pallas_call | solution.py:435
  20.4 5.6 %all-to-all-start = ((bf16[64,32,128]{2,1,0:T(8,128)(2,1)}), bf16[64,32,128]{2,1,0:T(8,128)(2,1)S(1)}, u32[]{:S(2)}, u32[]{:S(2)}) async-start(bf16[64,32,128]{2,1,0:T(8,128)(2,1)} %get-tuple-element.40), calls=%async_computation | async-start | bytes 1048576 | tf_op jit(solution)/shard_map/all_to_all | solution.py:447
  26.0 10.3 %collective-permute-done.1.mir_ref = bf16[16,8192]{1,0:T(8,128)(2,1)S(1)} collective-permute-done((bf16[16,8192]{1,0:T(8,128)(2,1)S(1)}, bf16[16,8192]{1,0:T(8,128)(2,1)S(1)}, u32[]{:S(2)}, u32[]{:S(2)}) %collective-permute-start.1) | collective-permute-done | bytes 262176 | tf_op jit(solution)/shard_map/ppermute | solution.py:30
  36.3 0.0 copy-start.5
  36.3 0.7 copy-done.5
  37.0 0.0 copy-done.1
  37.0 0.0 copy-done.2
  37.0 0.0 copy-done.4
  37.0 0.0 copy-done.7
  37.0 0.0 copy-start.6
  37.0 0.9 %copy-done.6 = bf16[16,8192]{1,0:T(8,128)(2,1)S(1)} copy-done((bf16[16,8192]{1,0:T(8,128)(2,1)S(1)}, bf16[16,8192]{1,0:T(8,128)(2,1)}, u32[]{:S(2)}) %copy-start.6) | copy-done | bytes 262168
  37.9 2.6 %shard_map.131.spec_ref = f32[1024,256]{1,0:T(8,128)S(1)} custom-call(f32[16,8192]{1,0:T(8,128)S(1)} %copy-done.1, bf16[16,8192]{1,0:T(8,128)(2,1)S(1)} %copy-done.6, f32[1024]{0:T(1024)S(1)} %copy-done.7, bf16[1024,256]{1,0:T(8,128)(2,1)S(1)} %copy-done.2, f32[2,64,128]{2,1,0:T(8,128)S(1)} %copy-done.4), custom_call_target="tpu_custom_call" | custom-call | flops 17179869184 | bytes 1835008 | tf_op jit(solution)/shard_map/pallas_call | solution.py:450
  40.5 3.0 %all-to-all-done.x_ref = bf16[64,32,128]{2,1,0:T(8,128)(2,1)S(1)} async-done(((bf16[64,32,128]{2,1,0:T(8,128)(2,1)}), bf16[64,32,128]{2,1,0:T(8,128)(2,1)S(1)}, u32[]{:S(2)}, u32[]{:S(2)}) %all-to-all-start) | async-done | bytes 524320 | tf_op jit(solution)/shard_map/all_to_all | solution.py:447
  43.6 1.9 %shard_map.132 = (f32[2048,256]{1,0:T(8,128)S(1)}, bf16[16,8192]{1,0:T(8,128)(2,1)S(1)}) custom-call(bf16[64,32,128]{2,1,0:T(8,128)(2,1)S(1)} %all-to-all-done.x_ref, bf16[1024,256]{1,0:T(8,128)(2,1)S(1)} %copy-done.2, f32[2,64,128]{2,1,0:T(8,128)S(1)} %copy-done.4), custom_call_target="tpu_custom_call" | custom-call | flops 536870912 | bytes 3145728 | tf_op jit(solution)/shard_map/pallas_call | solution.py:466
  45.5 5.8 %collective-permute-start.2 = (bf16[16,8192]{1,0:T(8,128)(2,1)S(1)}, bf16[16,8192]{1,0:T(8,128)(2,1)S(1)}, u32[]{:S(2)}, u32[]{:S(2)}) collective-permute-start(bf16[16,8192]{1,0:T(8,128)(2,1)S(1)} %get-tuple-element.50), channel_id=1, source_target_pairs={{0,255},{1,254},{2,253},{3,252},{4,251},{5,250},{6,249},{7,248},{8... | collective-permute-start | bytes 786440 | tf_op jit(solution)/shard_map/ppermute | solution.py:30
  51.2 2.6 %shard_map.133 = bf16[64,40,128]{2,1,0:T(8,128)(2,1)} custom-call(f32[2048,256]{1,0:T(8,128)S(1)} %get-tuple-element.43.spectra_ref, f32[1024,256]{1,0:T(8,128)S(1)} %shard_map.131.spec_ref, bf16[1024,256]{1,0:T(8,128)(2,1)S(1)} %copy-done.2, f32[2,64,128]{2,1,0:T(8,128)S(1)} %copy-done.4), custom_call_target="tpu_custom_call" | custom-call | flops 536870912 | bytes 3145728 | tf_op jit(solution)/shard_map/pallas_call | solution.py:482
  53.8 5.3 %all-to-all-start.1 = ((bf16[64,40,128]{2,1,0:T(8,128)(2,1)}), bf16[64,40,128]{2,1,0:T(8,128)(2,1)S(1)}, u32[]{:S(2)}, u32[]{:S(2)}) async-start(bf16[64,40,128]{2,1,0:T(8,128)(2,1)} %shard_map.133), calls=%async_computation.1 | async-start | bytes 1310720 | tf_op jit(solution)/shard_map/all_to_all | solution.py:496
  59.1 6.8 %collective-permute-done.2.far_ref = bf16[16,8192]{1,0:T(8,128)(2,1)S(1)} collective-permute-done((bf16[16,8192]{1,0:T(8,128)(2,1)S(1)}, bf16[16,8192]{1,0:T(8,128)(2,1)S(1)}, u32[]{:S(2)}, u32[]{:S(2)}) %collective-permute-start.2) | collective-permute-done | bytes 262176 | tf_op jit(solution)/shard_map/ppermute | solution.py:30
  65.9 0.0 copy-start
  65.9 0.0 copy-start.3
  65.9 1.4 %collective-permute-start.3 = (bf16[3,2,1024]{2,1,0:T(2,128)(2,1)S(1)}, bf16[3,2,1024]{2,1,0:T(2,128)(2,1)S(1)}, u32[]{:S(2)}, u32[]{:S(2)}) collective-permute-start(bf16[3,2,1024]{2,1,0:T(2,128)(2,1)S(1)} %get-tuple-element.51), channel_id=1, source_target_pairs={{4,0},{8,4},{12,8},{16,12},{20,16},{24,20},{28,24},{32,28},{36,32}... | collective-permute-start | bytes 36872 | tf_op jit(solution)/shard_map/ppermute | solution.py:25
  67.3 2.7 %shard_map.134 = f32[16,8192]{1,0:T(8,128)} custom-call(bf16[64,32,128]{2,1,0:T(8,128)(2,1)S(1)} %all-to-all-done.x_ref, bf16[16,8192]{1,0:T(8,128)(2,1)S(1)} %collective-permute-done.2.far_ref, bf16[1024,256]{1,0:T(8,128)(2,1)S(1)} %copy-done.2, f32[2,64,128]{2,1,0:T(8,128)S(1)} %copy-done.4), custom_call_target="tpu_custom_call" | custom-call | flops 17179869184 | bytes 1310720 | tf_op jit(solution)/shard_map/pallas_call | solution.py:500
  70.0 5.4 %collective-permute-done.3.next_ref = bf16[3,2,1024]{2,1,0:T(2,128)(2,1)S(1)} collective-permute-done((bf16[3,2,1024]{2,1,0:T(2,128)(2,1)S(1)}, bf16[3,2,1024]{2,1,0:T(2,128)(2,1)S(1)}, u32[]{:S(2)}, u32[]{:S(2)}) %collective-permute-start.3) | collective-permute-done | bytes 12320 | tf_op jit(solution)/shard_map/ppermute | solution.py:25
  75.5 5.0 %all-to-all-done.1.r_ref = bf16[64,40,128]{2,1,0:T(8,128)(2,1)S(1)} async-done(((bf16[64,40,128]{2,1,0:T(8,128)(2,1)}), bf16[64,40,128]{2,1,0:T(8,128)(2,1)S(1)}, u32[]{:S(2)}, u32[]{:S(2)}) %all-to-all-start.1) | async-done | bytes 655392 | tf_op jit(solution)/shard_map/all_to_all | solution.py:496
  80.5 0.0 copy-done
  80.5 0.0 copy-done.3
  80.5 1.6 %shard_map.135 = (bf16[128,1024]{1,0:T(8,128)(2,1)}, bf16[128,1024]{1,0:T(8,128)(2,1)}, bf16[128,1024]{1,0:T(8,128)(2,1)}, bf16[128,1024]{1,0:T(8,128)(2,1)}) custom-call(bf16[64,40,128]{2,1,0:T(8,128)(2,1)S(1)} %all-to-all-done.1.r_ref, bf16[128,1024]{1,0:T(8,128)(2,1)S(1)} %copy-done, bf16[128,1024]{1,0:T(8,128)(2,1)S(1)} %get-tuple-element.45.qs_ref, ...), custom_call_target="tpu_custom_call" | custom-call | flops 3932160 | bytes 2621440 | tf_op jit(solution)/shard_map/pallas_call | solution.py:514
Async XLA Ops:
  1.5 35.4 %copy-start.1 = (f32[16,8192]{1,0:T(8,128)S(1)}, f32[16,8192]{1,0:T(8,128)}, u32[]{:S(2)}) copy-start(f32[16,8192]{1,0:T(8,128)} %own_ref.1) | copy-start | bytes 1572868
  1.6 35.4 %copy-start.2 = (bf16[1024,256]{1,0:T(8,128)(2,1)S(1)}, bf16[1024,256]{1,0:T(8,128)(2,1)}, u32[]{:S(2)}) copy-start(bf16[1024,256]{1,0:T(8,128)(2,1)} %constant.4.clone.table_ref) | copy-start | bytes 1572868
  1.6 35.4 %copy-start.4 = (f32[2,64,128]{2,1,0:T(8,128)S(1)}, f32[2,64,128]{2,1,0:T(8,128)}, u32[]{:S(2)}) copy-start(f32[2,64,128]{2,1,0:T(8,128)} %constant.5.clone.twist_ref) | copy-start | bytes 196612
  1.6 35.4 %copy-start.7 = (f32[1024]{0:T(1024)S(1)}, f32[1024]{0:T(1024)}, u32[]{:S(2)}) copy-start(f32[1024]{0:T(1024)} %skip_ref.1) | copy-start | bytes 12292
  1.6 5.9 %collective-permute-start = (bf16[3,2,1024]{2,1,0:T(2,128)(2,1)S(1)}, bf16[3,2,1024]{2,1,0:T(2,128)(2,1)S(1)}, u32[]{:S(2)}, u32[]{:S(2)}) collective-permute-start(bf16[3,2,1024]{2,1,0:T(2,128)(2,1)S(1)} %get-tuple-element.37), channel_id=1, source_target_pairs={{0,4},{4,8},{8,12},{12,16},{16,20},{20,24},{24,28},{28,32},{32,36}... | collective-permute-start | bytes 36872 | tf_op jit(solution)/shard_map/ppermute | solution.py:25
  7.5 28.8 %collective-permute-start.1 = (bf16[16,8192]{1,0:T(8,128)(2,1)S(1)}, bf16[16,8192]{1,0:T(8,128)(2,1)S(1)}, u32[]{:S(2)}, u32[]{:S(2)}) collective-permute-start(bf16[16,8192]{1,0:T(8,128)(2,1)S(1)} %get-tuple-element.41), channel_id=1, source_target_pairs={{0,255},{1,254},{2,253},{3,252},{4,251},{5,250},{6,249},{7,248},{8... | collective-permute-start | bytes 786440 | tf_op jit(solution)/shard_map/ppermute | solution.py:30
  20.4 23.2 %all-to-all-start = ((bf16[64,32,128]{2,1,0:T(8,128)(2,1)}), bf16[64,32,128]{2,1,0:T(8,128)(2,1)S(1)}, u32[]{:S(2)}, u32[]{:S(2)}) async-start(bf16[64,32,128]{2,1,0:T(8,128)(2,1)} %get-tuple-element.40), calls=%async_computation | async-start | bytes 1048576 | tf_op jit(solution)/shard_map/all_to_all | solution.py:447
  36.3 0.7 copy-start.5
  37.0 1.0 %copy-start.6 = (bf16[16,8192]{1,0:T(8,128)(2,1)S(1)}, bf16[16,8192]{1,0:T(8,128)(2,1)}, u32[]{:S(2)}) copy-start(bf16[16,8192]{1,0:T(8,128)(2,1)} %copy-done.5) | copy-start | bytes 786436
  45.5 20.5 %collective-permute-start.2 = (bf16[16,8192]{1,0:T(8,128)(2,1)S(1)}, bf16[16,8192]{1,0:T(8,128)(2,1)S(1)}, u32[]{:S(2)}, u32[]{:S(2)}) collective-permute-start(bf16[16,8192]{1,0:T(8,128)(2,1)S(1)} %get-tuple-element.50), channel_id=1, source_target_pairs={{0,255},{1,254},{2,253},{3,252},{4,251},{5,250},{6,249},{7,248},{8... | collective-permute-start | bytes 786440 | tf_op jit(solution)/shard_map/ppermute | solution.py:30
  53.8 26.7 %all-to-all-start.1 = ((bf16[64,40,128]{2,1,0:T(8,128)(2,1)}), bf16[64,40,128]{2,1,0:T(8,128)(2,1)S(1)}, u32[]{:S(2)}, u32[]{:S(2)}) async-start(bf16[64,40,128]{2,1,0:T(8,128)(2,1)} %shard_map.133), calls=%async_computation.1 | async-start | bytes 1310720 | tf_op jit(solution)/shard_map/all_to_all | solution.py:496
  65.9 14.6 %copy-start = (bf16[128,1024]{1,0:T(8,128)(2,1)S(1)}, bf16[128,1024]{1,0:T(8,128)(2,1)}, u32[]{:S(2)}) copy-start(bf16[128,1024]{1,0:T(8,128)(2,1)} %g_ref.1) | copy-start | bytes 786436
  65.9 14.6 %copy-start.3 = (f32[3,3,1024]{2,1,0:T(4,128)S(1)}, f32[3,3,1024]{2,1,0:T(4,128)}, u32[]{:S(2)}) copy-start(f32[3,3,1024]{2,1,0:T(4,128)} %taps_ref.1) | copy-start | bytes 110596
  65.9 9.5 %collective-permute-start.3 = (bf16[3,2,1024]{2,1,0:T(2,128)(2,1)S(1)}, bf16[3,2,1024]{2,1,0:T(2,128)(2,1)S(1)}, u32[]{:S(2)}, u32[]{:S(2)}) collective-permute-start(bf16[3,2,1024]{2,1,0:T(2,128)(2,1)S(1)} %get-tuple-element.51), channel_id=1, source_target_pairs={{4,0},{8,4},{12,8},{16,12},{20,16},{24,20},{28,24},{32,28},{36,32}... | collective-permute-start | bytes 36872 | tf_op jit(solution)/shard_map/ppermute | solution.py:25
